TPU v7x, 128 devices: a whole 4x4x4 slice. The times are simulated.
128 devices in a mesh: ctx: 16 (over z, y), head: 8 (over x, core).
Axes of the slice: x: 4, y: 4, z: 4, core: 2. Of those that a mesh axis runs over, the one named last changes fastest.
Arguments:
- queries: bfloat16 [16384, 12288], P('ctx', 'head'), may hold values from -24 to 24
- key_rows: bfloat16 [16384, 768], P('ctx'), may hold values from -6 to 6
- value_rows: bfloat16 [16384, 512], P('ctx'), may hold values from -6 to 6
- comp_key_weight: float32 [32, 768], replicated, may hold values from 0.35355338 to 0.70710677
- comp_value_weight: float32 [32, 512], replicated, may hold values from 0.17677669 to 0.53033006
- block_picks: int32 [64, 4, 16], P('ctx'), may hold values from 0 to 252, as said below
- gate_logits: float32 [16384, 3, 64], P('ctx', None, 'head'), may hold values from -6 to 6
- out_weight: bfloat16 [8192, 2560], P('head'), may hold values from -0.25 to 0.25
Outputs:
- layer_out: bfloat16 [16384, 2560], P(('ctx', 'head'))
Inputs may be any that keep to these rules, and one draw needn't show every extreme that they name: `block_picks`: for each group, the lists of the 256-position query blocks held by one ctx shard name exactly 1024 / 256 distinct blocks of each earlier shard and of their own shard, and none of later shards; the own-shard blocks named are the first blocks of those query blocks. Every list names the first block of its own query block. Names may repeat within a list.
All inputs are finite; a program needn't handle non-finite values.
Results may differ from a plain program's by a relative error of at most 0.03.
Values may be sent and summed in bfloat16 or wider, within the bound.
A program may use at most 128 MiB of HBM per device.

v0:
```python
import jax
import jax.numpy as jnp
from jax import lax
from jax.sharding import PartitionSpec as P

HEADS = 64
GROUPS = 4
QUERY_KEY_WIDTH = 192
DV = 128
CBLK = 32
KBLK = 64
PICKS = 16
WINDOW = 512
QBLK = 256


NEG_FILL = -1e30


def shifted(block, axis, distance):
    devices = range(lax.axis_size(axis))
    route = [(i - distance, i) for i in devices if i - distance in devices]
    return lax.ppermute(block, axis, route)


def softmax_parts(scores, keep_mask):
    row_top = jnp.max(jnp.where(keep_mask, scores, NEG_FILL), axis=-1, keepdims=True)
    weights = jnp.where(keep_mask, jnp.exp(scores - row_top), 0.0)
    return (weights.astype(jnp.bfloat16), jnp.sum(weights, axis=-1))


def local(
    queries,
    key_rows,
    value_rows,
    comp_key_weight,
    comp_value_weight,
    block_picks,
    gate_logits,
    out_weight,
):
    tok_rows = queries.shape[0]
    heads_here = queries.shape[1] // QUERY_KEY_WIDTH
    shard_index = lax.axis_index("ctx")
    group_index = lax.axis_index("head") * heads_here // (HEADS // GROUPS)
    lane_count = QUERY_KEY_WIDTH + DV
    per_owner = tok_rows // KBLK
    query_blocks = tok_rows // QBLK
    score_scale = QUERY_KEY_WIDTH ** (-0.5)
    own_keys = lax.dynamic_slice_in_dim(key_rows, group_index * QUERY_KEY_WIDTH, QUERY_KEY_WIDTH, 1)
    own_values = lax.dynamic_slice_in_dim(value_rows, group_index * DV, DV, 1)
    packed = jnp.concatenate([own_keys, own_values], axis=1).reshape(per_owner, KBLK * lane_count)
    query_heads = queries.reshape(tok_rows, heads_here, QUERY_KEY_WIDTH)
    block_queries = queries.reshape(query_blocks, QBLK, heads_here, QUERY_KEY_WIDTH)
    positions = shard_index * tok_rows + jnp.arange(tok_rows, dtype=jnp.int32)
    query_pos = positions.reshape(query_blocks, QBLK)
    gates = jax.nn.sigmoid(gate_logits)
    key_weight = lax.dynamic_slice_in_dim(
        comp_key_weight, group_index * QUERY_KEY_WIDTH, QUERY_KEY_WIDTH, 1
    )
    value_weight = lax.dynamic_slice_in_dim(comp_value_weight, group_index * DV, DV, 1)
    comp_keys = jnp.sum(
        own_keys.reshape(tok_rows // CBLK, CBLK, QUERY_KEY_WIDTH).astype(jnp.float32)
        * key_weight[None],
        axis=1,
    ).astype(jnp.bfloat16)
    comp_values = jnp.sum(
        own_values.reshape(tok_rows // CBLK, CBLK, DV).astype(jnp.float32) * value_weight[None],
        axis=1,
    ).astype(jnp.bfloat16)
    all_comp_keys, all_comp_values = (
        lax.all_gather(comp_keys, "ctx", axis=0, tiled=True),
        lax.all_gather(comp_values, "ctx", axis=0, tiled=True),
    )
    comp_count = all_comp_keys.shape[0]
    comp_ends = (jnp.arange(comp_count, dtype=jnp.int32) + 1) * CBLK - 1
    row_span = min(512, tok_rows)

    def comp_span(span_index):
        first_row = span_index * row_span
        span_queries = lax.dynamic_slice_in_dim(query_heads, first_row, row_span, 0)
        span_pos = lax.dynamic_slice_in_dim(positions, first_row, row_span, 0)
        scores = (
            jnp.einsum(
                "thc,nc->thn", span_queries, all_comp_keys, preferred_element_type=jnp.float32
            )
            * score_scale
        )
        keep_mask = comp_ends[None, None, :] <= span_pos[:, None, None]
        weights, weight_sum = softmax_parts(scores, keep_mask)
        span_out = jnp.einsum(
            "thn,nd->thd", weights, all_comp_values, preferred_element_type=jnp.float32
        )
        return span_out / jnp.maximum(weight_sum, 1.0)[..., None]

    comp_out = lax.map(comp_span, jnp.arange(tok_rows // row_span, dtype=jnp.int32)).reshape(
        tok_rows, heads_here, DV
    )
    rim_rows = shifted(packed[per_owner - WINDOW // KBLK :], "ctx", 1)
    extended = jnp.concatenate([rim_rows, packed], axis=0).reshape(WINDOW + tok_rows, lane_count)
    window_spans = jnp.stack(
        [
            extended[span_index * QBLK : span_index * QBLK + WINDOW + QBLK]
            for span_index in range(query_blocks)
        ]
    )
    win_scores = (
        jnp.einsum(
            "bqhc,bkc->bqhk",
            block_queries,
            window_spans[..., :QUERY_KEY_WIDTH],
            preferred_element_type=jnp.float32,
        )
        * score_scale
    )
    key_pos = (
        shard_index * tok_rows
        - WINDOW
        + jnp.arange(query_blocks, dtype=jnp.int32)[:, None] * QBLK
        + jnp.arange(WINDOW + QBLK, dtype=jnp.int32)[None, :]
    )
    keep_mask = (
        (key_pos[:, None, :] >= 0)
        & (key_pos[:, None, :] <= query_pos[:, :, None])
        & (key_pos[:, None, :] >= query_pos[:, :, None] - WINDOW)
    )
    win_weights, win_sum = softmax_parts(win_scores, keep_mask[:, :, None, :])
    win_out = (
        jnp.einsum(
            "uzai,uix->uzax",
            win_weights,
            window_spans[..., QUERY_KEY_WIDTH:],
            preferred_element_type=jnp.float32,
        )
        / win_sum[..., None]
    )
    my_picks = lax.dynamic_index_in_dim(block_picks, group_index, 1, keepdims=False)
    flat_picks = my_picks.reshape(query_blocks * PICKS)
    gathered = lax.all_gather(packed, "ctx", axis=0, tiled=True)
    tiled_row_groups = gathered[flat_picks]
    tiled_row_groups = tiled_row_groups.reshape(query_blocks, PICKS * KBLK, lane_count)
    pick_order = jnp.arange(PICKS, dtype=jnp.int32)
    repeated = jnp.any(
        (my_picks[:, :, None] == my_picks[:, None, :])
        & (pick_order[None, None, :] < pick_order[None, :, None]),
        axis=-1,
    )
    pick_pos = (my_picks[:, :, None] * KBLK + jnp.arange(KBLK, dtype=jnp.int32)).reshape(
        query_blocks, PICKS * KBLK
    )
    live_mask = jnp.repeat(jnp.logical_not(repeated), KBLK, axis=1)
    keep_mask = (pick_pos[:, None, :] <= query_pos[:, :, None]) & live_mask[:, None, :]
    sel_scores = (
        jnp.einsum(
            "bqhc,bkc->bqhk",
            block_queries,
            tiled_row_groups[..., :QUERY_KEY_WIDTH],
            preferred_element_type=jnp.float32,
        )
        * score_scale
    )
    selected_weights, selected_sum = softmax_parts(sel_scores, keep_mask[:, :, None, :])
    sel_out = (
        jnp.einsum(
            "uzai,uix->uzax",
            selected_weights,
            tiled_row_groups[..., QUERY_KEY_WIDTH:],
            preferred_element_type=jnp.float32,
        )
        / selected_sum[..., None]
    )
    mixed = (
        gates[:, 0, :, None] * comp_out
        + gates[:, 1, :, None] * sel_out.reshape(tok_rows, heads_here, DV)
        + gates[:, 2, :, None] * win_out.reshape(tok_rows, heads_here, DV)
    )
    attended = mixed.astype(jnp.bfloat16).reshape(tok_rows, heads_here * DV)
    return lax.psum_scatter(
        jnp.dot(attended, out_weight, preferred_element_type=jnp.float32).astype(jnp.bfloat16),
        "head",
        scatter_dimension=0,
        tiled=True,
    )


def solution(mesh):
    placed = (
        P("ctx", "head"),
        P("ctx", None),
        P("ctx", None),
        P(),
        P(),
        P("ctx", None, None),
        P("ctx", None, "head"),
        P("head", None),
    )
    return jax.shard_map(
        local, mesh=mesh, in_specs=placed, out_specs=P(("ctx", "head"), None), check_vma=False
    )
```

profile of v0, /device:TPU:0, one launch (start us, length us, event | category | flops | bytes accessed | tf_op | source)
XLA Modules:
  0.0 297.4 jit_solution(15637494506940244456)
XLA Ops:
  6.5 1.4 copy-done
  9.9 1.7 reshape.226
  11.9 1.1 slice.53
  13.0 4.3 %collective-permute-start = (bf16[8,20480]{1,0:T(8,128)(2,1)}, bf16[8,20480]{1,0:T(8,128)(2,1)}, u32[]{:S(2)}, u32[]{:S(2)}) collective-permute-start(bf16[8,20480]{1,0:T(8,128)(2,1)} %slice.53), channel_id=1, source_target_pairs={{0,8},{8,16},{16,24},{24,32},{32,40},{40,48},{48,56},{56,64},{64,7... | collective-permute-start | bytes 983048 | tf_op jit(solution)/shard_map/ppermute | solution.py:23
  17.3 1.0 fusion.75
  20.9 1.2 copy.75
  24.1 1.3 fusion.85
  26.5 3.2 %copy.73 = bf16[1024,1536]{0,1:T(8,128)(2,1)S(1)} copy(bf16[1024,1536]{1,0:T(8,128)(2,1)} %param.10) | data formatting | bytes 6291456 | tf_op args[0]
  30.6 1.4 multiply_reduce_fusion
  32.0 26.6 %all_gather.9 = bf16[512,192]{1,0:T(8,128)(2,1)} all-gather(bf16[32,192]{1,0:T(8,128)(2,1)S(1)} %multiply_reduce_fusion), channel_id=1, replica_groups=mesh['ctx'=16,'head'=8] {'ctx'}, dimensions={0}, use_global_device_ids=true | all-gather | bytes 208896 | tf_op jit(solution)/shard_map/all_gather | solution.py:72
  58.6 1.1 copy.78
  60.4 1.1 multiply_reduce_fusion.1
  61.5 22.3 %all_gather.10 = bf16[512,128]{1,0:T(8,128)(2,1)S(1)} all-gather(bf16[32,128]{1,0:T(8,128)(2,1)S(1)} %multiply_reduce_fusion.1), channel_id=1, replica_groups=mesh['ctx'=16,'head'=8] {'ctx'}, dimensions={0}, use_global_device_ids=true | all-gather | bytes 139264 | tf_op jit(solution)/shard_map/all_gather | solution.py:73
  85.9 3.0 compare_and_fusion.1
  89.3 30.3 %while.11 = (s32[]{:T(128)}, f32[2,512,8,128]{3,2,1,0:T(8,128)}, s32[2]{0:T(128)}, s32[1024]{0:T(1024)}, bf16[1024,8,192]{0,2,1:T(8,128)(2,1)S(1)}, /*index=5*/b...) while((s32[]{:T(128)}, f32[2,512,8,128]{3,2,1,0:T(8,128)}, ...), condition=%wide.region_5.6_spmd.clone, body=%wide.region_2.5_spmd.clone.sunk | while | flops 1357649920 | bytes 33974984 | solution.py:96
  89.3 1.2 dynamic_slice.46
  91.1 1.4 fusion.112
  92.9 5.5 %fusion.113 = (f32[512,8]{0,1:T(8,128)S(1)}, bf16[512,8,512]{0,2,1:T(8,128)(2,1)}) fusion(f32[512,8,512]{0,2,1:T(8,128)S(1)} %fusion.112, pred[512,512]{0,1:T(8,128)(4,1)S(1)} %broadcast_compare_fusion.3), kind=kOutput, calls=%fused_computation.122.clone.1 | output fusion | flops 14680575 | bytes 12861440 | tf_op jit(solution)/shard_map/while/body/eval_jaxpr/sub | solution.py:28
  98.4 3.4 %divide_bitcast_fusion.2 = f32[1,512,8,128]{3,1,2,0:T(8,128)S(1)} fusion(bf16[512,8,512]{0,2,1:T(8,128)(2,1)} %get-tuple-element.158, f32[512,8]{0,1:T(8,128)S(1)} %broadcast_maximum_fusion.2, bf16[512,128]{1,0:T(8,128)(2,1)S(1)} %get-tuple-element.188), kind=kOutput, calls=%fused_computation.13.clone.1 | convolution fusion | flops 537395200 | bytes 6438912 | tf_op jit(solution)/shard_map/while/body/eval_jaxpr/thn,nd->thd/dot_general | solution.py:91
  101.9 2.6 copy_dynamic-update-slice_fusion.2
  104.5 1.2 dynamic_slice.46
  106.3 1.5 fusion.112
  108.1 5.5 %fusion.113 = (f32[512,8]{0,1:T(8,128)S(1)}, bf16[512,8,512]{0,2,1:T(8,128)(2,1)}) fusion(f32[512,8,512]{0,2,1:T(8,128)S(1)} %fusion.112, pred[512,512]{0,1:T(8,128)(4,1)S(1)} %broadcast_compare_fusion.3), kind=kOutput, calls=%fused_computation.122.clone.1 | output fusion | flops 14680575 | bytes 12861440 | tf_op jit(solution)/shard_map/while/body/eval_jaxpr/sub | solution.py:28
  113.6 3.4 %divide_bitcast_fusion.2 = f32[1,512,8,128]{3,1,2,0:T(8,128)S(1)} fusion(bf16[512,8,512]{0,2,1:T(8,128)(2,1)} %get-tuple-element.158, f32[512,8]{0,1:T(8,128)S(1)} %broadcast_maximum_fusion.2, bf16[512,128]{1,0:T(8,128)(2,1)S(1)} %get-tuple-element.188), kind=kOutput, calls=%fused_computation.13.clone.1 | convolution fusion | flops 537395200 | bytes 6438912 | tf_op jit(solution)/shard_map/while/body/eval_jaxpr/thn,nd->thd/dot_general | solution.py:91
  117.0 2.6 copy_dynamic-update-slice_fusion.2
  120.3 3.9 %reshape.229 = bf16[4,256,8,192]{1,0,3,2:T(4,128)(2,1)} reshape(bf16[1024,1536]{0,1:T(8,128)(2,1)S(1)} %bitcast.144) | data formatting | bytes 6291456 | tf_op jit(solution)/shard_map/reshape | solution.py:54
  126.4 1.0 copy.87
  127.4 3.3 %compare_and_fusion = pred[4,256,1024]{1,2,0:T(8,128)(4,1)} fusion(s32[4,256]{1,0:T(4,128)S(1)} %copy-done.8, s32[4,1024]{1,0:T(4,128)S(1)} %broadcast_add_fusion, pred[4,1024]{1,0:T(4,128)(4,1)S(1)} %and.51), kind=kLoop, calls=%fused_computation.55 | loop fusion | flops 2097152 | bytes 1073152 | tf_op jit(solution)/shard_map/and | solution.py:152
  131.7 1.1 constant_dynamic-update-slice_fusion
  132.9 1.3 fusion.87
  134.2 2.8 stack.15
  136.9 2.1 copy.89
  139.0 2.6 stack.16
  141.6 2.1 copy.90
  143.7 3.0 pad_maximum_fusion
  146.7 15.7 %fusion.88 = (f32[4,256,8]{1,2,0:T(8,128)S(1)}, bf16[4,256,8,768]{1,3,2,0:T(8,128)(2,1)}) fusion(pred[4,256,768]{1,2,0:T(8,128)(4,1)} %compare_and_fusion.1, bf16[4,256,8,192]{1,0,3,2:T(4,128)(2,1)S(1)} %copy-done.2, bf16[4,768,320]{1,2,0:T(8,128)(2,1)} %pad_maximum_fusion), kind=kOutput, calls=%fused_computation.124 | convolution fusion | flops 4875878912 | bytes 22839296 | tf_op jit(solution)/shard_map/sub | solution.py:28
  162.4 8.1 %broadcast_divide_fusion = f32[4,256,8,128]{3,1,2,0:T(8,128)S(1)} fusion(f32[4,256,8]{1,2,0:T(8,128)S(1)} %get-tuple-element.103, bf16[4,256,8,768]{1,3,2,0:T(8,128)(2,1)} %get-tuple-element.104, bf16[1,768,320]{1,2,0:T(8,128)(2,1)} %get-tuple-element.99, bf16[1,768,320]{1,2,0:T(8,128)(2,1)} %get-tuple-element.98, bf16[1,768,320]{1,2,0:T(8,128)(2,1)} %copy.90, ...), kind=kOutput, calls=%fused_computation.61 | convolution fusion | flops 1614807040 | bytes 18776064 | tf_op jit(solution)/shard_map/uzai,uix->uzax/dot_general | solution.py:129
  170.5 4.5 %copy.94 = f32[4,256,8,128]{3,2,1,0:T(8,128)} copy(f32[4,256,8,128]{3,1,2,0:T(8,128)S(1)} %broadcast_divide_fusion) | data formatting | bytes 8388608 | tf_op jit(solution)/shard_map/div | solution.py:129
  175.0 9.8 %gather_fusion = bf16[64,20480]{1,0:T(8,128)(2,1)S(1)} fusion(bf16[256,20480]{1,0:T(8,128)(2,1)} %all-gather.2.cloned.1.call-done, s32[1024]{0:T(1024)S(1)} %pad_clamp_fusion), kind=kCustom, calls=%fused_computation | custom fusion | bytes 5243136 | tf_op jit(solution)/shard_map/gather | solution.py:140
  184.8 4.7 %reshape.228 = bf16[4,1024,320]{2,1,0:T(8,128)(2,1)} reshape(bf16[64,20480]{1,0:T(8,128)(2,1)S(1)} %gather_fusion) | data formatting | bytes 5242880 | tf_op jit(solution)/shard_map/reshape | solution.py:141
  189.4 20.7 %fusion.93 = (f32[4,256,8]{1,2,0:T(8,128)S(1)}, bf16[4,256,8,1024]{1,3,2,0:T(8,128)(2,1)}) fusion(pred[4,256,1024]{1,2,0:T(8,128)(4,1)} %compare_and_fusion, bf16[4,256,8,192]{1,0,3,2:T(4,128)(2,1)} %reshape.229, bf16[4,1024,320]{2,1,0:T(8,128)(2,1)} %reshape.228), kind=kOutput, calls=%fused_computation.125 | convolution fusion | flops 6501172224 | bytes 29392896 | tf_op jit(solution)/shard_map/sub | solution.py:28
  210.1 11.4 %fusion.46 = f32[4,256,8,128]{3,1,2,0:T(8,128)S(1)} fusion(bf16[4,256,8,1024]{1,3,2,0:T(8,128)(2,1)} %get-tuple-element.106, f32[4,256,8]{1,2,0:T(8,128)S(1)} %get-tuple-element.105, bf16[4,1024,320]{2,1,0:T(8,128)(2,1)} %reshape.228), kind=kOutput, calls=%fused_computation.58 | convolution fusion | flops 2148532224 | bytes 22052864 | tf_op jit(solution)/shard_map/uzai,uix->uzax/dot_general | solution.py:164
  221.5 4.4 %copy.86 = f32[4,256,8,128]{3,2,1,0:T(8,128)} copy(f32[4,256,8,128]{3,1,2,0:T(8,128)S(1)} %fusion.46) | data formatting | bytes 8388608 | tf_op jit(solution)/shard_map/div | solution.py:164
  225.9 1.1 mul.123
  227.1 1.1 mul.137
  228.2 2.9 mul.146
  231.2 19.5 %convolution_convert_fusion = bf16[1024,2560]{1,0:T(8,128)(2,1)} fusion(bf16[1024,2560]{1,0:T(8,128)(2,1)} %param.17, f32[128,8,8,128]{3,2,1,0:T(8,128)} %bitcast.148, f32[128,8,8,128]{3,2,1,0:T(8,128)} %bitcast.147, f32[128,8,8,128]{3,2,1,0:T(8,128)} %bitcast.149, f32[128,8,8,128]{3,2,1,0:T(8,128)S(1)} %bitcast.146, f32[128,8,8,128]{3,2,1,0:T(8,128)} %bitcast.32, ...), kind=kOutput, calls=%fused_computation.48 | convolution fusion | flops 5377622016 | bytes 35651584 | tf_op jit(solution)/shard_map/dot_general | solution.py:179
  250.7 39.7 %reduce-scatter.2.cloned.1.call-done = bf16[128,2560]{1,0:T(8,128)(2,1)} async-done(((bf16[1024,2560]{1,0:T(8,128)(2,1)}), bf16[128,2560]{1,0:T(8,128)(2,1)}) %reduce-scatter.2.cloned.1.call-update) | async-done | bytes 655376 | tf_op jit(solution)/shard_map/reduce_scatter | solution.py:178
  (74 shorter events, 16.5 us)
Async XLA Ops:
  6.5 1.4 copy-start
  6.5 168.4 %all-gather.2.cloned.1.call-start = ((), (), s32[]{:S(2)}) async-start(), calls=%async_computation.1 | async-start | bytes 11141120 | tf_op jit(solution)/shard_map/all_gather | solution.py:139
  11.6 278.8 %reduce-scatter.2.cloned.1.call-start = ((), (), s32[]{:S(2)}) async-start(), calls=%async_computation.2 | async-start | bytes 5898240 | tf_op jit(solution)/shard_map/reduce_scatter | solution.py:178
  13.0 117.7 %collective-permute-start = (bf16[8,20480]{1,0:T(8,128)(2,1)}, bf16[8,20480]{1,0:T(8,128)(2,1)}, u32[]{:S(2)}, u32[]{:S(2)}) collective-permute-start(bf16[8,20480]{1,0:T(8,128)(2,1)} %slice.53), channel_id=1, source_target_pairs={{0,8},{8,16},{16,24},{24,32},{32,40},{40,48},{48,56},{56,64},{64,7... | collective-permute-start | bytes 983048 | tf_op jit(solution)/shard_map/ppermute | solution.py:23
  91.1 1.4 copy-start.7
  106.3 1.5 copy-start.7
  119.7 4.6 %copy-start.9 = (pred[4,16]{1,0:T(4,128)(4,1)S(1)}, pred[4,16]{1,0:T(4,128)(4,1)}, u32[]{:S(2)}) copy-start(pred[4,16]{1,0:T(4,128)(4,1)} %and_reduce_fusion) | copy-start | bytes 196
  119.7 4.7 %copy-start.6 = (f32[1024,8]{0,1:T(8,128)S(1)}, f32[1024,8]{0,1:T(8,128)}, u32[]{:S(2)}) copy-start(f32[1024,8]{0,1:T(8,128)} %get-tuple-element.100) | copy-start | bytes 98308
  119.7 7.8 %copy-start.8 = (s32[4,256]{1,0:T(4,128)S(1)}, s32[4,256]{1,0:T(4,128)}, u32[]{:S(2)}) copy-start(s32[4,256]{1,0:T(4,128)} %add_add_fusion) | copy-start | bytes 12292
  134.2 12.5 %copy-start.2 = (bf16[4,256,8,192]{1,0,3,2:T(4,128)(2,1)S(1)}, bf16[4,256,8,192]{1,0,3,2:T(4,128)(2,1)}, u32[]{:S(2)}) copy-start(bf16[4,256,8,192]{1,0,3,2:T(4,128)(2,1)} %reshape.229) | copy-start | bytes 9437188
  221.5 4.5 %copy-start.3 = (f32[1024,8]{1,0:T(8,128)S(1)}, f32[1024,8]{1,0:T(8,128)}, u32[]{:S(2)}) copy-start(f32[1024,8]{1,0:T(8,128)} %copy.72) | copy-start | bytes 98308
  225.9 1.1 copy-start.4
  225.9 2.3 copy-start.5
  231.2 59.2 %copy-start.1 = (bf16[1024,768]{1,0:T(8,128)(2,1)S(1)}, bf16[1024,768]{1,0:T(8,128)(2,1)}, u32[]{:S(2)}) copy-start(bf16[1024,768]{1,0:T(8,128)(2,1)} %param.11) | copy-start | bytes 4718596
Sparse Core Ops, SparseCore 0:
  11.7 84.1 all-gather.1
  250.8 39.5 reduce-scatter.1
where the time goes:
time: 302 us; the launch traced here: 297 us
  matrix products  85.1 us (28%)
  local copies, waits for them, and re-layouts  74 us (25%)
  blocking collectives  48.9 us (16%)
  waiting for transfers between devices  39.7 us (13%)
  other arithmetic  30.4 us (10%)
  between operations  13.8 us (5%)
  starting transfers between devices  4.33 us (1%)
    reduce_scatter x1, waiting for transfers between devices, local(): lax.psum_scatter(jnp.dot(attended, out_weight, preferred_element_type=jnp...  39.7 us
    sub x2, matrix products, softmax_parts(): weights = jnp.where(keep_mask, jnp.exp(scores - row_top), 0.0)  36.3 us
    all_gather x1, blocking collectives, local(): lax.all_gather(comp_keys, 'ctx', axis=0, tiled=True)  26.6 us
    all_gather x1, blocking collectives, local(): lax.all_gather(comp_values, 'ctx', axis=0, tiled=True)  22.3 us
    dot_general x1, matrix products, local(): jnp.dot(attended, out_weight, preferred_element_type=jnp.float32)  19.5 us
    dot_general x1, matrix products, local(): jnp.einsum('uzai,uix->uzax', selected_weights, tiled_row_groups[..., QUER...  11.4 us
    sub x2, other arithmetic, softmax_parts(): weights = jnp.where(keep_mask, jnp.exp(scores - row_top), 0.0)  11.1 us
    gather x1, local copies, waits for them, and re-layouts, local(): tiled_row_groups = gathered[flat_picks]  9.79 us
  transfers between devices with their start and end apart: 3, of which 1 were waited for; matrix products, arithmetic and copies ran while one was open for 37% of the time, Pallas kernels for 0%

commit v1 on v0

v1 whole, which is shorter than its diff:
```python
import functools, math
import jax, jax.numpy as jnp
from jax import lax
from jax.experimental import pallas as pl
from jax.experimental.pallas import tpu as pltpu

QK=192; DV=128; CBLK=32; KBLK=64; PICKS=16; WINDOW=512; QBLK=256
DEAD=-1e30; FLOOR=-1e20
SCALE2=QK**-0.5*math.log2(math.e)
BF=jnp.bfloat16; F32=jnp.float32

def nt(a,b):
    return lax.dot_general(a,b,(((1,),(1,)),((),())),preferred_element_type=F32)

def branch(q,k,v,bias):
    s=nt(q,k)+bias
    top=jnp.maximum(jnp.max(s,axis=1,keepdims=True),FLOOR)
    w=jnp.exp2((s-top)*SCALE2).astype(BF)
    acc=jnp.dot(w,v,preferred_element_type=F32)
    return acc[:,:DV],acc[:,DV:]

def body(shard_ref,slot_ref,q_ref,gate_ref,bias_s_ref,own_ref,rim_ref,comp_ref,blk_ref,w_ref,o_ref,
         ke,ko,vx,ce,co,cx,se,so,sx,bw,bc,bs,att):
    qb=pl.program_id(0)
    shard=shard_ref[0]
    rows=lax.broadcasted_iota(jnp.int32,(QBLK,QBLK),0)
    cols=lax.broadcasted_iota(jnp.int32,(QBLK,QBLK),1)

    @pl.when(qb==0)
    def _():
        vx[:,DV:]=jnp.ones((vx.shape[0],DV),BF)
        cx[:,DV:]=jnp.ones((cx.shape[0],DV),BF)
        sx[:,DV:]=jnp.ones((sx.shape[0],DV),BF)
        def put(src,n,base):
            def one(i,_):
                x=src[i]
                r=pl.ds(pl.multiple_of(base+i*KBLK,KBLK),KBLK)
                ke[r,:]=x[:,:256]
                ko[r,:]=pltpu.roll(x[:,:256].astype(F32),64,1).astype(BF)
                vx[r,:DV]=x[:,256:]
                return 0
            lax.fori_loop(0,n,one,0)
        put(rim_ref,8,0)
        put(own_ref,16,WINDOW)
        def onec(i,_):
            x=comp_ref[i]
            r=pl.ds(pl.multiple_of(i*CBLK,CBLK),CBLK)
            ce[r,:]=x[:,:256]
            co[r,:]=pltpu.roll(x[:,:256].astype(F32),64,1).astype(BF)
            cx[r,:DV]=x[:,256:]
            return 0
        lax.fori_loop(0,16,onec,0)

    def ones(j,_):
        x=blk_ref[slot_ref[qb*PICKS+j]]
        r=pl.ds(pl.multiple_of(j*KBLK,KBLK),KBLK)
        se[r,:]=x[:,:256]
        so[r,:]=pltpu.roll(x[:,:256].astype(F32),64,1).astype(BF)
        sx[r,:DV]=x[:,256:]
        return 0
    lax.fori_loop(0,PICKS,ones,0)
    first=shard*1024+qb*QBLK
    b0=jnp.where(first<512,DEAD,0.0)
    b1=jnp.where(first<256,DEAD,0.0)
    bw[:,:256]=jnp.where(cols>=rows,b0,DEAD)
    bw[:,256:512]=jnp.full((QBLK,QBLK),b1)
    bw[:,512:]=jnp.where(cols<=rows,0.0,DEAD)
    rowc=lax.broadcasted_iota(jnp.int32,(QBLK,512),0)
    colc=lax.broadcasted_iota(jnp.int32,(QBLK,512),1)
    bc[...]=jnp.where(colc<32,jnp.where(colc*32+31<=qb*QBLK+rowc,0.0,DEAD),jnp.where(colc<(shard+1)*32,0.0,DEAD))
    rs=lax.broadcasted_iota(jnp.int32,(QBLK,1024),0)
    cs=lax.broadcasted_iota(jnp.int32,(QBLK,1024),1)
    bs[...]=jnp.where((cs<64)&(cs>rs),DEAD,jnp.broadcast_to(bias_s_ref[...].reshape(1,1024),(QBLK,1024)))
    gl=gate_ref[...]
    gates=1.0/(1.0+jnp.exp(-gl))
    gates=jnp.concatenate([gates,jnp.zeros((104,QBLK),F32)],axis=0).T
    wr=pl.ds(pl.multiple_of(qb*QBLK,QBLK),768)
    for h in range(8):
        off=(h//2)*384+(h%2)*128
        q=q_ref[:,off:off+256]
        K,C,S=(ko,co,so) if h%2 else (ke,ce,se)
        nc,dc=branch(q,C[...],cx[...],bc[...])
        ns,ds_=branch(q,S[...],sx[...],bs[...])
        nw,dw=branch(q,K[wr,:],vx[wr,:],bw[...])
        out=(gates[:,h:h+1]/jnp.maximum(dc,1.0))*nc+(gates[:,8+h:9+h]/ds_)*ns+(gates[:,16+h:17+h]/dw)*nw
        att[:,h*DV:(h+1)*DV]=out.astype(BF)
    o_ref[...]=jnp.dot(att[...],w_ref[...],preferred_element_type=F32).astype(BF)

def attend(shard,slots,q,gate,bias_s,own,rim,comp,blk,w):
    one=lambda shape: pl.BlockSpec(shape,lambda i,*_:(0,)*len(shape),pipeline_mode=pl.Buffered(1))
    return pl.pallas_call(body,
        grid_spec=pltpu.PrefetchScalarGridSpec(num_scalar_prefetch=2,grid=(4,),
        in_specs=[pl.BlockSpec((QBLK,1536),lambda i,*_:(i,0)),
                  pl.BlockSpec((24,QBLK),lambda i,*_:(0,i)),
                  pl.BlockSpec((None,1,1024),lambda i,*_:(i,0,0)),
                  one((16,64,384)),one((8,64,384)),one((16,32,384)),one((64,64,384)),one((1024,2560))],
        out_specs=pl.BlockSpec((QBLK,2560),lambda i,*_:(i,0)),
        scratch_shapes=[pltpu.VMEM((1536,256),BF)]*3+[pltpu.VMEM((512,256),BF)]*3+[pltpu.VMEM((1024,256),BF)]*3
          +[pltpu.VMEM((QBLK,768),F32),pltpu.VMEM((QBLK,512),F32),pltpu.VMEM((QBLK,1024),F32),pltpu.VMEM((QBLK,1024),BF)]),
        out_shape=jax.ShapeDtypeStruct((1024,2560),BF),
        compiler_params=pltpu.CompilerParams(vmem_limit_bytes=56<<20),
    )(shard,slots,q,gate,bias_s,own,rim,comp,blk,w)
import functools, math
import jax, jax.numpy as jnp
from jax import lax
from jax.experimental import pallas as pl
from jax.experimental.pallas import tpu as pltpu
MESH=pl.DeviceIdType.MESH
I32=jnp.int32

def plan(picks,shard):
    pos=lax.broadcasted_iota(I32,(4,PICKS),1)
    own=shard*16+4*lax.broadcasted_iota(I32,(4,PICKS),0)
    at=jnp.min(jnp.where(picks==own,pos,PICKS),axis=1,keepdims=True)
    p=jnp.where(pos==0,own,jnp.where(pos==at,picks[:,0:1],picks))
    row=jnp.concatenate([p[i:i+1] for i in range(4)]+[jnp.full((1,64),-1,I32)],axis=1)
    pr=jnp.broadcast_to(row,(128,128))
    pc=pr.astype(F32).T.astype(I32)
    ri=lax.broadcasted_iota(I32,(128,128),0)
    ci=lax.broadcasted_iota(I32,(128,128),1)
    one=lambda x: jnp.where(x,1.0,0.0)
    same=pr==pc
    dup=jnp.sum(one(same&(ri<ci)&((ri>>4)==(ci>>4))),axis=0,keepdims=True)
    new_r=jnp.where((jnp.sum(one(same&(ri<ci)),axis=0,keepdims=True)==0)&(ci[:1]<64),1.0,0.0)
    new_c=jnp.where((jnp.sum(one(same&(ci<ri)),axis=1,keepdims=True)==0)&(ri[:,:1]<64),1.0,0.0)
    mates=(pr>>4)==(pc>>4)
    rank_r=jnp.sum(jnp.where(mates&(pc<pr),new_c,0.0),axis=0,keepdims=True).astype(I32)
    rank_c=jnp.sum(jnp.where(mates&(pr<pc),new_r,0.0),axis=1,keepdims=True).astype(I32)
    slot_r=(row>>4)*4+rank_r
    slot_c=(pc[:,:1]>>4)*4+rank_c
    req=jnp.sum(jnp.where(slot_c==ci,new_c,0.0)*(pc&15).astype(F32),axis=0,keepdims=True).astype(I32)
    dead=jnp.where((dup>0)|(row>shard*16+4*(ci[:1]>>4))|(ci[:1]>=64),1.0,0.0)
    return req,slot_r,dead

def exch(picks_ref,key_ref,val_ref,kw_ref,vw_ref,
         slot_out,bias_out,own_out,rim_out,comp_out,blk_out,
         kbuf,vbuf,pk,crow,zero,reqb,reqin,send,reqs,
         ksem,lsem,rq_s,rq_r,rim_s,rim_r,cp_s,cp_r,bk_s,bk_r,sm_s):
    me=lax.axis_index("ctx"); g=lax.axis_index("head")//2
    n=16
    bar=pltpu.get_barrier_semaphore()
    def hi(i,_):
        pl.semaphore_signal(bar,inc=1,device_id={"ctx":(me+i)%n},device_id_type=MESH)
        return 0
    lax.fori_loop(1,n,hi,0)
    odd=g%2
    ck=pltpu.make_async_copy(key_ref.at[:,pl.ds(pl.multiple_of((g//2)*384,128),384)],kbuf,ksem.at[0])
    cv=pltpu.make_async_copy(val_ref.at[:,pl.ds(pl.multiple_of(g*DV,128),DV)],vbuf,ksem.at[1])
    ck.start(); cv.start()
    req,slot,dead=plan(picks_ref[:,g,:],me)
    reqb[...]=jnp.broadcast_to(req,(8,128))
    slot_out[...]=slot
    ei=lax.broadcasted_iota(I32,(128,1024),0)
    ej=lax.broadcasted_iota(I32,(128,1024),1)
    d8=jnp.broadcast_to(dead,(8,128))
    for qb in range(4):
        m=jnp.dot(d8,jnp.where(ei==qb*16+(ej>>6),1.0,0.0),preferred_element_type=F32)
        bias_out[qb]=jnp.where(m[:1]>0.5,DEAD,0.0)
    pl.semaphore_wait(bar,n-1)
    def rq(o): return pltpu.make_async_remote_copy(reqb,reqin.at[me],rq_s.at[o],rq_r.at[me],device_id={"ctx":o},device_id_type=MESH)
    def rqin(t): return pltpu.make_async_remote_copy(reqb,reqin.at[t],rq_s.at[t],rq_r.at[t],device_id={"ctx":t},device_id_type=MESH)
    lax.fori_loop(0,me,lambda o,_:(rq(o).start(),0)[1],0)
    ck.wait(); cv.wait()
    lane=lax.broadcasted_iota(I32,(KBLK,256),1)
    oddv=(lane>=0)&(lane*0+odd>0)
    keep=(lane>=odd*64)&(lane<QK+odd*64)
    kwr=kw_ref.at[:,pl.ds(pl.multiple_of((g//2)*384,128),384)]
    wk=jnp.where(oddv[:CBLK],kwr[:,128:384],kwr[:,0:256])
    wv=vw_ref[:,pl.ds(pl.multiple_of(g*DV,128),DV)]
    def pack(i,_):
        r=pl.ds(pl.multiple_of(i*KBLK,KBLK),KBLK)
        x=jnp.where(oddv,kbuf[r,128:384].astype(F32),kbuf[r,0:256].astype(F32))
        x=jnp.where(keep,x,0.0)
        x=jnp.where(oddv,pltpu.roll(x,192,1),x)
        v=vbuf[r,:]
        pk[i,:,:256]=x.astype(BF)
        pk[i,:,256:]=v
        return 0
    lax.fori_loop(0,16,pack,0)
    wk2=jnp.where(oddv[:CBLK],pltpu.roll(wk,192,1),wk)
    for b in range(32):
        r=slice((b%2)*32,(b%2)*32+32)
        crow[b:b+1,:256]=jnp.sum(pk[b//2,r,:256].astype(F32)*wk2,axis=0,keepdims=True)
        crow[b:b+1,256:]=jnp.sum(pk[b//2,r,256:].astype(F32)*wv,axis=0,keepdims=True)
    zero[...]=crow[...].astype(BF)
    def cp(t): return pltpu.make_async_remote_copy(zero,comp_out.at[t-me],cp_s.at[t-me],cp_r.at[t-me],device_id={"ctx":t},device_id_type=MESH)
    def cpin(d): return pltpu.make_async_remote_copy(zero,comp_out.at[d],cp_s.at[d],cp_r.at[d],device_id={"ctx":(me+d)%n},device_id_type=MESH)
    rim=pltpu.make_async_remote_copy(pk.at[pl.ds(8,8)],rim_out,rim_s,rim_r,device_id={"ctx":(me+1)%n},device_id_type=MESH)
    @pl.when(me<n-1)
    def _(): rim.start()
    lax.fori_loop(me+1,n,lambda t,_:(cp(t).start(),0)[1],0)
    own=pltpu.make_async_copy(pk,own_out,lsem.at[0]); own.start()
    firsts=[pltpu.make_async_copy(pk.at[4*i],blk_out.at[me*4+i],lsem.at[1+i]) for i in range(4)]
    for f in firsts: f.start()
    ownc=pltpu.make_async_copy(zero,comp_out.at[0],lsem.at[5]); ownc.start()
    def sm(t): return pltpu.make_async_copy(reqin.at[t],reqs.at[t],sm_s.at[t])
    def take(t,_):
        rqin(t).wait_recv(); sm(t).start(); return 0
    lax.fori_loop(me+1,n,take,0)
    def bk(t): return pltpu.make_async_remote_copy(send.at[t],blk_out.at[pl.ds(me*4,4)],bk_s.at[t],bk_r.at[me],device_id={"ctx":t},device_id_type=MESH)
    def bkin(o): return pltpu.make_async_remote_copy(send.at[o],blk_out.at[pl.ds(o*4,4)],bk_s.at[o],bk_r.at[o],device_id={"ctx":o},device_id_type=MESH)
    def give(t,_):
        sm(t).wait()
        for j in range(4):
            send[t,j]=pk[reqs[t,0,me*4+j]&15]
        bk(t).start()
        return 0
    lax.fori_loop(me+1,n,give,0)
    own.wait(); ownc.wait()
    for f in firsts: f.wait()
    @pl.when(me<n-1)
    def _(): rim.wait_send()
    @pl.when(me>0)
    def _(): rim.wait_recv()
    lax.fori_loop(0,me,lambda o,_:(rq(o).wait_send(),0)[1],0)
    lax.fori_loop(me+1,n,lambda t,_:(cp(t).wait_send(),0)[1],0)
    lax.fori_loop(me+1,n,lambda t,_:(bk(t).wait_send(),0)[1],0)
    lax.fori_loop(1,me+1,lambda d,_:(cpin(d).wait_recv(),0)[1],0)
    zero[...]=jnp.zeros_like(zero)
    def blank(d,_):
        c=pltpu.make_async_copy(zero,comp_out.at[d],lsem.at[6]); c.start(); c.wait(); return 0
    lax.fori_loop(me+1,n,blank,0)
    @pl.when(me==0)
    def _():
        pk[pl.ds(0,8)]=jnp.zeros((8,KBLK,384),BF)
        c=pltpu.make_async_copy(pk.at[pl.ds(0,8)],rim_out,lsem.at[6]); c.start(); c.wait()
    lax.fori_loop(0,me,lambda o,_:(bkin(o).wait_recv(),0)[1],0)

def exchange(picks,keys,vals,kw,vw):
    vm=pl.BlockSpec(memory_space=pltpu.VMEM); hb=pl.BlockSpec(memory_space=pl.ANY)
    S=jax.ShapeDtypeStruct; D=pltpu.SemaphoreType.DMA
    return pl.pallas_call(exch,
        in_specs=[vm,hb,hb,vm,vm],out_specs=[vm,vm,hb,hb,hb,hb],
        out_shape=[S((1,128),I32),S((4,1,1024),F32),S((16,64,384),BF),S((8,64,384),BF),S((16,32,384),BF),S((64,64,384),BF)],
        scratch_shapes=[pltpu.VMEM((1024,384),BF),pltpu.VMEM((1024,DV),BF),pltpu.VMEM((16,64,384),BF),pltpu.VMEM((32,384),F32),
            pltpu.VMEM((32,384),BF),pltpu.VMEM((8,128),I32),pltpu.VMEM((16,8,128),I32),pltpu.VMEM((16,4,64,384),BF),pltpu.SMEM((16,8,128),I32),
            D((2,)),D((7,)),D((16,)),D((16,)),D,D,D((16,)),D((16,)),D((16,)),D((16,)),D((16,))],
        compiler_params=pltpu.CompilerParams(collective_id=0,has_side_effects=True,vmem_limit_bytes=40<<20),
    )(picks,keys,vals,kw,vw)

def local(queries,key_rows,value_rows,kw,vw,picks,gate,w):
    shard=lax.axis_index("ctx").reshape(1)
    slot,bias,own,rim,comp,blk=exchange(picks,key_rows,value_rows,kw,vw)
    part=attend(shard,slot[0,:64],queries,gate.transpose(1,2,0).reshape(24,1024),bias,own,rim,comp,blk,w)
    return lax.psum_scatter(part,"head",scatter_dimension=0,tiled=True)

from jax.sharding import PartitionSpec as P
def solution(mesh):
    placed=(P("ctx","head"),P("ctx",None),P("ctx",None),P(),P(),P("ctx",None,None),P("ctx",None,"head"),P("head",None))
    return jax.shard_map(local,mesh=mesh,in_specs=placed,out_specs=P(("ctx","head"),None),check_vma=False)
```

time: 302 us -> 179 us (0.59)
  the two profiles are of different devices: /device:TPU:0 before, /device:TPU:71 now
where the time goes in v1:
time: 179 us; the launch traced here: 176 us
  Pallas kernels  112 us (63%)
  waiting for transfers between devices  40.6 us (23%)
  between operations  13.4 us (7%)
  local copies, waits for them, and re-layouts  10.3 us (6%)
    pallas_call x1, Pallas kernels, attend(): pl.pallas_call(body, grid_spec=pltpu.PrefetchScalarGridSpec(num_scalar_pr...  56.4 us
    pallas_call x1, Pallas kernels, exchange(): pl.pallas_call(exch, in_specs=[vm, hb, hb, vm, vm], out_specs=[vm, vm, hb...  55.7 us
    reduce_scatter x1, waiting for transfers between devices, local(): return lax.psum_scatter(part, 'head', scatter_dimension=0, tiled=True)  40.5 us
    unnamed x20, local copies, waits for them, and re-layouts  9.75 us
  transfers between devices with their start and end apart: 1, of which 1 were waited for; matrix products, arithmetic and copies ran while one was open for 0% of the time, Pallas kernels for 0%

profile of v1, /device:TPU:71, one launch (start us, length us, event | category | flops | bytes accessed | tf_op | source)
XLA Modules:
  0.0 176.4 jit_solution(6911623265131287489)
XLA Ops:
  6.5 0.0 reduce-scatter.2.cloned.1.call-start
  6.5 0.0 copy-start.1
  6.5 1.4 copy-done.1
  7.9 0.0 copy-start.2
  7.9 1.2 copy-done.2
  9.2 0.0 copy-start.6
  9.2 0.9 copy-done.6
  10.1 0.0 copy-start.7
  10.1 0.8 copy-done.7
  10.9 0.0 copy-start.9
  10.9 0.7 copy-done.9
  11.6 55.7 %shard_map.82 = (s32[1,128]{1,0:T(1,128)S(1)}, f32[4,1,1024]{2,1,0:T(1,128)S(1)}, bf16[16,64,384]{2,1,0:T(8,128)(2,1)S(1)}, bf16[8,64,384]{2,1,0:T(8,128)(2,1)S(...) custom-call(s32[4,4,16]{2,1,0:T(4,128)S(1)} %copy-done.9, bf16[1024,768]{1,0:T(8,128)(2,1)S(1)} %copy-done.1, ...), custom_call_target="tpu_custom_call" | custom-call | tf_op jit(solution)/shard_map/pallas_call | solution.py:232
  67.3 0.0 copy-start
  67.3 1.6 copy-done
  69.0 0.0 copy-start.3
  69.0 1.0 copy-done.3
  69.9 0.0 copy-start.4
  69.9 0.7 copy-done.4
  70.7 0.0 copy-start.5
  70.7 0.8 copy-done.5
  71.4 0.0 copy-start.8
  71.4 0.6 copy-done.8
  72.0 0.5 slice_bitcast_fusion.slot_ref
  72.5 56.4 %shard_map.83 = bf16[1024,2560]{1,0:T(8,128)(2,1)} custom-call(s32[1]{0:T(128)} %bitcast.shard_ref, s32[64]{0:T(128)} %slice_bitcast_fusion.slot_ref, bf16[1024,1536]{1,0:T(8,128)(2,1)} %q_ref.1, f32[24,1024]{1,0:T(8,128)} %bitcast.6, f32[4,1,1024]{2,1,0:T(1,128)} %copy-done.8, bf16[16,64,384]{2,1,0:T(8,128)(2,1)} %copy-done.3, ...), custom_call_target="tpu_custom_call" | custom-call | tf_op jit(solution)/shard_map/pallas_call | solution.py:91
  128.9 0.0 reduce-scatter.2.cloned.1.call-update
  129.0 40.5 %reduce-scatter.2.cloned.1.call-done = bf16[128,2560]{1,0:T(8,128)(2,1)} async-done(((bf16[1024,2560]{1,0:T(8,128)(2,1)}), bf16[128,2560]{1,0:T(8,128)(2,1)}) %reduce-scatter.2.cloned.1.call-update) | async-done | bytes 655376 | tf_op jit(solution)/shard_map/reduce_scatter | solution.py:245
Async XLA Ops:
  6.5 163.0 %reduce-scatter.2.cloned.1.call-start = ((), (), s32[]{:S(2)}) async-start(), calls=%async_computation.1 | async-start | bytes 5898240 | tf_op jit(solution)/shard_map/reduce_scatter | solution.py:245
  6.5 1.4 copy-start.1
  7.9 1.2 copy-start.2
  9.2 0.9 copy-start.6
  10.1 0.8 copy-start.7
  10.9 0.7 copy-start.9
  67.3 1.7 copy-start
  69.0 1.0 copy-start.3
  69.9 0.7 copy-start.4
  70.7 0.8 copy-start.5
  71.4 0.6 copy-start.8
Sparse Core Ops, SparseCore 0:
  129.1 40.3 reduce-scatter.1

commit v2 on v0

v2 whole, which is shorter than its diff:
```python
import math

import jax
import jax.numpy as jnp
from jax import lax
from jax.experimental import pallas as pl
from jax.experimental.pallas import tpu as pltpu
from jax.sharding import PartitionSpec as P

QK = 192
DV = 128
CBLK = 32
KBLK = 64
PICKS = 16
WINDOW = 512
QBLK = 256
N_CTX = 16
DEAD = -1e30
FLOOR = -1e20
SCALE2 = QK**-0.5 * math.log2(math.e)
BF = jnp.bfloat16
F32 = jnp.float32
I32 = jnp.int32
MESH = pl.DeviceIdType.MESH
HALF = 1280


def one(x):
    return jnp.where(x, 1.0, 0.0)


def iota(shape, axis):
    return lax.broadcasted_iota(I32, shape, axis)


def plan(picks, shard):
    pos = iota((4, PICKS), 1)
    own = shard * 16 + 4 * iota((4, PICKS), 0)
    at = jnp.min(jnp.where(picks == own, pos, PICKS), axis=1, keepdims=True)
    p = jnp.where(pos == 0, own, jnp.where(pos == at, picks[:, 0:1], picks))
    row = jnp.concatenate([p[i : i + 1] for i in range(4)] + [jnp.full((1, 64), -1, I32)], axis=1)
    pr = jnp.broadcast_to(row, (128, 128))
    pc = pr.astype(F32).T.astype(I32)
    ri = iota((128, 128), 0)
    ci = iota((128, 128), 1)
    same = pr == pc
    dup = jnp.sum(one(same & (ri < ci) & ((ri >> 4) == (ci >> 4))), axis=0, keepdims=True)
    new_r = one((jnp.sum(one(same & (ri < ci)), axis=0, keepdims=True) == 0) & (ci[:1] < 64))
    new_c = one((jnp.sum(one(same & (ci < ri)), axis=1, keepdims=True) == 0) & (ri[:, :1] < 64))
    mates = (pr >> 4) == (pc >> 4)
    rank_r = jnp.sum(jnp.where(mates & (pc < pr), new_c, 0.0), axis=0, keepdims=True).astype(I32)
    rank_c = jnp.sum(jnp.where(mates & (pr < pc), new_r, 0.0), axis=1, keepdims=True).astype(I32)
    slot_r = (row >> 4) * 4 + rank_r
    slot_c = (pc[:, :1] >> 4) * 4 + rank_c
    req = jnp.sum(jnp.where(slot_c == ci, new_c, 0.0) * (pc & 15).astype(F32), axis=0, keepdims=True)
    dead = one((dup > 0) | (row > shard * 16 + 4 * (ci[:1] >> 4)) | (ci[:1] >= 64))
    return req.astype(I32), slot_r, dead


def branch(q, k, v, bias):
    s = lax.dot_general(q, k, (((1,), (1,)), ((), ())), preferred_element_type=F32) + bias
    top = jnp.maximum(jnp.max(s, axis=1, keepdims=True), FLOOR)
    w = jnp.exp2((s - top) * SCALE2).astype(BF)
    acc = jnp.dot(w, v, preferred_element_type=F32)
    return acc[:, :DV], acc[:, DV:]


def each(lo, hi, act):
    def step(i, carry):
        act(i)
        return carry

    lax.fori_loop(lo, hi, step, 0)


def layer(
    q_hbm, key_hbm, val_hbm, kw_hbm, vw_hbm, picks_hbm, gate_hbm, w_hbm, o_hbm,
    q, kbuf, vbuf, kw, vw, picks, gate, w, gt,
    pk, crow, cown, reqb, reqin, reqs, slotb, slots, send, blk, comp, rim,
    ke, ko, vx, ce, co, cx, se, so, sx, bw, bc, bs, rowb, acc, att,
    mine, psend, precv, sa, ra, sb, rb, outb,
    lsem, sm_s, rq_s, rq_r, rim_s, rim_r, cp_s, cp_r, bk_s, bk_r, fw_s, fw_r, pr_s, pr_r, a_s, a_r, b_s, b_r,
):
    me = lax.axis_index("ctx")
    head = lax.axis_index("head")
    x = head // 2
    core = head % 2
    g = x
    odd = g % 2
    n = N_CTX
    sib = {"head": x * 2 + 1 - core}
    up = {"head": ((x + 1) % 4) * 2 + core}
    down = {"head": ((x + 3) % 4) * 2 + core}

    def remote(src, dst, ss, rs, dev):
        return pltpu.make_async_remote_copy(src, dst, ss, rs, device_id=dev, device_id_type=MESH)

    bar = pltpu.get_barrier_semaphore()
    each(1, n, lambda i: pl.semaphore_signal(bar, inc=1, device_id={"ctx": (me + i) % n}, device_id_type=MESH))
    for dev in (sib, up, down):
        pl.semaphore_signal(bar, inc=1, device_id=dev, device_id_type=MESH)

    loads = [
        pltpu.make_async_copy(picks_hbm, picks, lsem.at[0]),
        pltpu.make_async_copy(key_hbm.at[:, pl.ds(pl.multiple_of((g // 2) * 384, 128), 384)], kbuf, lsem.at[1]),
        pltpu.make_async_copy(val_hbm.at[:, pl.ds(pl.multiple_of(g * DV, 128), DV)], vbuf, lsem.at[2]),
        pltpu.make_async_copy(kw_hbm.at[:, pl.ds(pl.multiple_of((g // 2) * 384, 128), 384)], kw, lsem.at[3]),
        pltpu.make_async_copy(vw_hbm.at[:, pl.ds(pl.multiple_of(g * DV, 128), DV)], vw, lsem.at[4]),
        pltpu.make_async_copy(gate_hbm, gate, lsem.at[5]),
        pltpu.make_async_copy(q_hbm, q, lsem.at[6]),
        pltpu.make_async_copy(w_hbm, w, lsem.at[7]),
    ]
    for c in loads:
        c.start()

    loads[0].wait()
    req, slot, dead = plan(picks[:, g, :], me)
    reqb[...] = jnp.broadcast_to(req, (8, 128))
    slotb[...] = jnp.broadcast_to(slot, (8, 128))
    to_s = pltpu.make_async_copy(slotb, slots, lsem.at[8])
    to_s.start()
    pl.semaphore_wait(bar, n - 1 + 3)

    def rq(o):
        return remote(reqb, reqin.at[me], rq_s.at[o], rq_r.at[me], {"ctx": o})

    def rq_in(t):
        return remote(reqb, reqin.at[t], rq_s.at[t], rq_r.at[t], {"ctx": t})

    each(0, me, lambda o: rq(o).start())

    ei = iota((128, 1024), 0)
    ej = iota((128, 1024), 1)
    d8 = jnp.broadcast_to(dead, (8, 128))
    for qb in range(4):
        m = jnp.dot(d8, one(ei == qb * 16 + (ej >> 6)), preferred_element_type=F32)
        rowb[qb] = jnp.where(m > 0.5, DEAD, 0.0)

    for c in loads[1:5]:
        c.wait()
    lane = iota((KBLK, 256), 1)
    oddv = (lane >= 0) & (lane * 0 + odd > 0)
    keep = (lane >= odd * 64) & (lane < QK + odd * 64)
    vx[:, DV:] = jnp.ones((vx.shape[0], DV), BF)
    cx[:, DV:] = jnp.ones((cx.shape[0], DV), BF)
    sx[:, DV:] = jnp.ones((sx.shape[0], DV), BF)

    def spread(block, rows, even_ref, odd_ref, v_ref):
        even_ref[rows, :] = block[:, :256]
        odd_ref[rows, :] = pltpu.roll(block[:, :256].astype(F32), 64, 1).astype(BF)
        v_ref[rows, :DV] = block[:, 256:]

    def pack(i):
        r = pl.ds(pl.multiple_of(i * KBLK, KBLK), KBLK)
        y = jnp.where(oddv, kbuf[r, 128:384].astype(F32), kbuf[r, 0:256].astype(F32))
        y = jnp.where(keep, y, 0.0)
        y = jnp.where(oddv, pltpu.roll(y, 192, 1), y).astype(BF)
        pk[i, :, :256] = y
        pk[i, :, 256:] = vbuf[r, :]
        r2 = pl.ds(pl.multiple_of(WINDOW + i * KBLK, KBLK), KBLK)
        spread(pk[i], r2, ke, ko, vx)

    each(0, 16, pack)
    rim_c = remote(pk.at[pl.ds(8, 8)], rim, rim_s, rim_r, {"ctx": (me + 1) % n})

    @pl.when(me < n - 1)
    def _():
        rim_c.start()

    wk = jnp.where(oddv[:CBLK], kw[:, 128:384], kw[:, 0:256])
    wk = jnp.where(oddv[:CBLK], pltpu.roll(wk, 192, 1), wk)
    wv = vw[...]
    for b in range(32):
        r = slice((b % 2) * 32, (b % 2) * 32 + 32)
        crow[b : b + 1, :256] = jnp.sum(pk[b // 2, r, :256].astype(F32) * wk, axis=0, keepdims=True)
        crow[b : b + 1, 256:] = jnp.sum(pk[b // 2, r, 256:].astype(F32) * wv, axis=0, keepdims=True)
    cown[...] = crow[...].astype(BF)

    def cp(t):
        return remote(cown, comp.at[t - me], cp_s.at[t - me], cp_r.at[t - me], {"ctx": t})

    def cp_in(d):
        return remote(cown, comp.at[d], cp_s.at[d], cp_r.at[d], {"ctx": (me + d) % n})

    each(me + 1, n, lambda t: cp(t).start())

    def sm(t):
        return pltpu.make_async_copy(reqin.at[t], reqs.at[t], sm_s.at[t])

    def take(t):
        rq_in(t).wait_recv()
        sm(t).start()

    each(me + 1, n, take)

    def bk(t):
        return remote(send.at[t], blk.at[pl.ds(me * 4 + 2 * core, 2)], bk_s.at[t], bk_r.at[me], {"ctx": t})

    def bk_in(o):
        return remote(send.at[o], blk.at[pl.ds(o * 4 + 2 * core, 2)], bk_s.at[o], bk_r.at[o], {"ctx": o})

    def fw(o):
        part = blk.at[pl.ds(o * 4 + 2 * core, 2)]
        return remote(part, part, fw_s.at[o], fw_r.at[o], sib)

    def fw_in(o):
        part = blk.at[pl.ds(o * 4 + 2 - 2 * core, 2)]
        return remote(part, part, fw_s.at[o], fw_r.at[o], sib)

    def give(t):
        sm(t).wait()
        for j in range(2):
            send[t, j] = pk[reqs[t, 0, me * 4 + 2 * core + j] & 15]
        bk(t).start()

    each(me + 1, n, give)

    def pass_on(o):
        bk_in(o).wait_recv()
        fw(o).start()

    loads[5].wait()
    for qb in range(4):
        sg = 1.0 / (1.0 + jnp.exp(-gate[:, qb * QBLK : (qb + 1) * QBLK]))
        gt[qb * QBLK : (qb + 1) * QBLK, :] = jnp.concatenate([sg, jnp.zeros((104, QBLK), F32)], axis=0).T
    for i in range(4):
        blk[me * 4 + i] = pk[4 * i]
    comp[0] = cown[...]

    def blank(d):
        comp[d] = jnp.zeros((CBLK, 384), BF)

    each(me + 1, n, blank)

    @pl.when(me == 0)
    def _():
        rim[...] = jnp.zeros_like(rim)

    @pl.when(me > 0)
    def _():
        rim_c.wait_recv()

    each(1, me + 1, lambda d: cp_in(d).wait_recv())
    each(0, 8, lambda i: spread(rim[i], pl.ds(pl.multiple_of(i * KBLK, KBLK), KBLK), ke, ko, vx))
    each(0, 16, lambda i: spread(comp[i], pl.ds(pl.multiple_of(i * CBLK, CBLK), CBLK), ce, co, cx))
    loads[6].wait()
    rows = iota((QBLK, QBLK), 0)
    cols = iota((QBLK, QBLK), 1)

    def near(qb):
        base = pl.multiple_of(qb * QBLK, QBLK)
        first = me * 1024 + base
        bw[:, :256] = jnp.where(cols >= rows, jnp.where(first < 512, DEAD, 0.0), DEAD)
        bw[:, 256:512] = jnp.full((QBLK, QBLK), jnp.where(first < 256, DEAD, 0.0))
        bw[:, 512:] = jnp.where(cols <= rows, 0.0, DEAD)
        rowc = iota((QBLK, 512), 0)
        colc = iota((QBLK, 512), 1)
        bc[...] = jnp.where(
            colc < 32,
            jnp.where(colc * 32 + 31 <= base + rowc, 0.0, DEAD),
            jnp.where(colc < (me + 1) * 32, 0.0, DEAD),
        )

        def pair(p):
            gr = pltpu.roll(gt[pl.ds(base, QBLK), :], 128 - 2 * p, 1)
            for par, K, C in ((0, ke, ce), (1, ko, co)):
                qh = q[pl.ds(base, QBLK), pl.ds(pl.multiple_of(p * 384 + par * 128, 128), 256)]
                nc, dc = branch(qh, C[...], cx[...], bc[...])
                nw, dw = branch(qh, K[pl.ds(base, 768), :], vx[pl.ds(base, 768), :], bw[...])
                acc[pl.ds(base, QBLK), pl.ds(pl.multiple_of(p * 256 + par * 128, 128), DV)] = (
                    gr[:, par : par + 1] / jnp.maximum(dc, 1.0)
                ) * nc + (gr[:, 16 + par : 17 + par] / dw) * nw

        each(0, 4, pair)

    def far_setup(qb):
        def put(j):
            r = pl.ds(pl.multiple_of(j * KBLK, KBLK), KBLK)
            spread(blk[slots[0, qb * PICKS + j] & 63], r, se, so, sx)

        each(0, PICKS, put)
        rs = iota((QBLK, 1024), 0)
        cs = iota((QBLK, 1024), 1)
        bs[...] = jnp.where((cs < 64) & (cs > rs), DEAD, jnp.broadcast_to(rowb[qb][0:1, :], (QBLK, 1024)))

    def far(qb, lo, hi):
        base = pl.multiple_of(qb * QBLK, QBLK)

        def pair(p):
            gr = pltpu.roll(gt[pl.ds(base, QBLK), :], 128 - 2 * p, 1)
            for par, S in ((0, se), (1, so)):
                qh = q[pl.ds(base, QBLK), pl.ds(pl.multiple_of(p * 384 + par * 128, 128), 256)]
                ns, ds = branch(qh, S[...], sx[...], bs[...])
                c = pl.ds(pl.multiple_of(p * 256 + par * 128, 128), DV)
                att[:, c] = (acc[pl.ds(base, QBLK), c] + (gr[:, 8 + par : 9 + par] / ds) * ns).astype(BF)

        each(lo, hi, pair)

    def pr(r):
        return remote(psend.at[r], precv.at[r], pr_s.at[r], pr_r.at[r], sib)

    def project(r):
        keep_rows = pl.ds(pl.multiple_of(core * 128, 128), 128)
        give_rows = pl.ds(pl.multiple_of(128 - core * 128, 128), 128)
        a = att[give_rows, :]
        b = att[keep_rows, :]

        def tile(i):
            c = pl.ds(pl.multiple_of(i * 256, 256), 256)
            psend[r, :, c] = jnp.dot(a, w[:, c], preferred_element_type=F32).astype(BF)
            mine[r, :, c] = jnp.dot(b, w[:, c], preferred_element_type=F32)

        each(0, 10, tile)
        pr(r).start()

    A = slice(0, HALF)
    B = slice(HALF, 2 * HALF)

    def total(r, c):
        return mine[r, :, c] + precv[r, :, c].astype(F32)

    def hop_a(k):
        return remote(sa.at[k], ra.at[k], a_s.at[k], a_r.at[k], up)

    def hop_b(k):
        return remote(sb.at[k], rb.at[k], b_s.at[k], b_r.at[k], down)

    order = [(x + 3) % 4, (x + 1) % 4, (x + 2) % 4, x]
    each(0, 2, lambda r: near(jnp.where(r == 0, order[0], order[1])))
    half = me // 2
    each(half, me, pass_on)
    near(order[2])
    each(0, half, pass_on)
    loads[7].wait()
    to_s.wait()
    each(0, me, lambda o: fw_in(o).wait_recv())

    far_setup(order[0])
    far(order[0], 0, 4)
    project(0)
    far_setup(order[1])
    far(order[1], 0, 2)
    pr(0).wait_recv()
    sa[0] = total(0, A).astype(BF)
    hop_a(0).start()
    far(order[1], 2, 4)
    project(1)
    far_setup(order[2])
    far(order[2], 0, 2)
    pr(1).wait_recv()
    sb[0] = total(1, B).astype(BF)
    hop_b(0).start()
    far(order[2], 2, 4)
    project(2)
    near(order[3])
    pr(2).wait_recv()
    hop_a(0).wait_recv()
    sa[1] = (total(2, A) + ra[0].astype(F32)).astype(BF)
    hop_a(1).start()
    hop_b(0).wait_recv()
    sb[1] = (total(2, B) + rb[0].astype(F32)).astype(BF)
    hop_b(1).start()
    far_setup(order[3])
    far(order[3], 0, 4)
    hop_a(1).wait_recv()
    sa[2] = (total(1, A) + ra[1].astype(F32)).astype(BF)
    hop_a(2).start()
    hop_b(1).wait_recv()
    sb[2] = (total(0, B) + rb[1].astype(F32)).astype(BF)
    hop_b(2).start()
    project(3)
    pr(3).wait_recv()
    hop_a(2).wait_recv()
    outb[:, A] = (total(3, A) + ra[2].astype(F32)).astype(BF)
    hop_b(2).wait_recv()
    outb[:, B] = (total(3, B) + rb[2].astype(F32)).astype(BF)
    done = pltpu.make_async_copy(outb, o_hbm, lsem.at[9])
    done.start()

    each(0, me, lambda o: rq(o).wait_send())
    each(me + 1, n, lambda t: cp(t).wait_send())
    each(me + 1, n, lambda t: bk(t).wait_send())
    each(0, me, lambda o: fw(o).wait_send())

    @pl.when(me < n - 1)
    def _():
        rim_c.wait_send()

    for r in range(4):
        pr(r).wait_send()
    for k in range(3):
        hop_a(k).wait_send()
        hop_b(k).wait_send()
    done.wait()


def local(queries, key_rows, value_rows, kw, vw, picks, gate, w):
    hbm = pl.BlockSpec(memory_space=pl.ANY)
    V = pltpu.VMEM
    D = pltpu.SemaphoreType.DMA
    return pl.pallas_call(
        layer,
        in_specs=[hbm] * 8,
        out_specs=hbm,
        out_shape=jax.ShapeDtypeStruct((128, 2560), BF),
        scratch_shapes=[
            V((1024, 1536), BF), V((1024, 384), BF), V((1024, DV), BF), V((CBLK, 384), F32), V((CBLK, DV), F32),
            V((4, 4, PICKS), I32), V((24, 1024), F32), V((1024, 2560), BF), V((1024, 128), F32),
            V((16, 64, 384), BF), V((32, 384), F32), V((32, 384), BF), V((8, 128), I32), V((16, 8, 128), I32),
            pltpu.SMEM((16, 8, 128), I32), V((8, 128), I32), pltpu.SMEM((8, 128), I32),
            V((16, 2, 64, 384), BF), V((64, 64, 384), BF), V((16, 32, 384), BF), V((8, 64, 384), BF),
            V((1536, 256), BF), V((1536, 256), BF), V((1536, 256), BF),
            V((512, 256), BF), V((512, 256), BF), V((512, 256), BF),
            V((1024, 256), BF), V((1024, 256), BF), V((1024, 256), BF),
            V((QBLK, 768), F32), V((QBLK, 512), F32), V((QBLK, 1024), F32), V((4, 8, 1024), F32),
            V((1024, 1024), F32), V((QBLK, 1024), BF),
            V((4, 128, 2560), F32), V((4, 128, 2560), BF), V((4, 128, 2560), BF),
            V((3, 128, HALF), BF), V((3, 128, HALF), BF), V((3, 128, HALF), BF), V((3, 128, HALF), BF),
            V((128, 2560), BF),
            D((10,)), D((16,)), D((16,)), D((16,)), D, D, D((16,)), D((16,)), D((16,)), D((16,)), D((16,)), D((16,)),
            D((4,)), D((4,)), D((3,)), D((3,)), D((3,)), D((3,)),
        ],
        compiler_params=pltpu.CompilerParams(
            collective_id=0, has_side_effects=True, vmem_limit_bytes=60 << 20
        ),
    )(queries, key_rows, value_rows, kw, vw, picks, gate.transpose(1, 2, 0).reshape(24, 1024), w)


def solution(mesh):
    placed = (
        P("ctx", "head"), P("ctx", None), P("ctx", None), P(), P(),
        P("ctx", None, None), P("ctx", None, "head"), P("head", None),
    )
    return jax.shard_map(
        local, mesh=mesh, in_specs=placed, out_specs=P(("ctx", "head"), None), check_vma=False
    )
```

time: 302 us -> 117 us (0.39)
  the two profiles are of different devices: /device:TPU:0 before, /device:TPU:71 now
where the time goes in v2:
time: 117 us; the launch traced here: 116 us
  Pallas kernels  114 us (97%)
  local copies, waits for them, and re-layouts  1.97 us (2%)
    pallas_call x1, Pallas kernels, local(): pl.pallas_call(layer, in_specs=[hbm] * 8, out_specs=hbm, out_shape=jax.Sh...  114 us

profile of v2, /device:TPU:71, one launch (start us, length us, event | category | flops | bytes accessed | tf_op | source)
XLA Modules:
  0.0 116.1 jit_solution(17773491628655149926)
XLA Ops:
  0.0 114.1 %shard_map.82 = bf16[128,2560]{1,0:T(8,128)(2,1)} custom-call(bf16[1024,1536]{1,0:T(8,128)(2,1)} %q_hbm.1, bf16[1024,768]{1,0:T(8,128)(2,1)} %key_hbm.1, bf16[1024,512]{1,0:T(8,128)(2,1)} %val_hbm.1, f32[32,768]{1,0:T(8,128)} %kw_hbm.1, f32[32,512]{1,0:T(8,128)} %vw_hbm.1, s32[4,4,16]{2,1,0:T(4,128)} %picks_hbm.1, f32[24,1024]{1,0:T(8,128)} %bitcast.3, ...), custom_call_target="tpu_custom_call" | custom-call | tf_op jit(solution)/shard_map/pallas_call | solution.py:401
  114.1 2.0 %copy.10 = bf16[128,2560]{1,0:T(8,128)(2,1)} copy(bf16[128,2560]{1,0:T(8,128)(2,1)} %shard_map.82) | data formatting | bytes 1310720

commit v3 on v2

--- a/solution.py
+++ b/solution.py
@@ -261,17 +261,17 @@
             jnp.where(colc < (me + 1) * 32, 0.0, DEAD),
         )
 
-        def pair(p):
-            gr = pltpu.roll(gt[pl.ds(base, QBLK), :], 128 - 2 * p, 1)
-            for par, K, C in ((0, ke, ce), (1, ko, co)):
-                qh = q[pl.ds(base, QBLK), pl.ds(pl.multiple_of(p * 384 + par * 128, 128), 256)]
-                nc, dc = branch(qh, C[...], cx[...], bc[...])
-                nw, dw = branch(qh, K[pl.ds(base, 768), :], vx[pl.ds(base, 768), :], bw[...])
-                acc[pl.ds(base, QBLK), pl.ds(pl.multiple_of(p * 256 + par * 128, 128), DV)] = (
-                    gr[:, par : par + 1] / jnp.maximum(dc, 1.0)
-                ) * nc + (gr[:, 16 + par : 17 + par] / dw) * nw
-
-        each(0, 4, pair)
+        r = pl.ds(base, QBLK)
+        span = pl.ds(base, 768)
+        for h in range(8):
+            off = (h // 2) * 384 + (h % 2) * 128
+            qh = q[r, off : off + 256]
+            K, C = (ko, co) if h % 2 else (ke, ce)
+            nc, dc = branch(qh, C[...], cx[...], bc[...])
+            nw, dw = branch(qh, K[span, :], vx[span, :], bw[...])
+            acc[r, h * DV : (h + 1) * DV] = (gt[r, h : h + 1] / jnp.maximum(dc, 1.0)) * nc + (
+                gt[r, 16 + h : 17 + h] / dw
+            ) * nw
 
     def far_setup(qb):
         def put(j):
@@ -283,41 +283,37 @@
         cs = iota((QBLK, 1024), 1)
         bs[...] = jnp.where((cs < 64) & (cs > rs), DEAD, jnp.broadcast_to(rowb[qb][0:1, :], (QBLK, 1024)))
 
-    def far(qb, lo, hi):
+    def far(qb):
         base = pl.multiple_of(qb * QBLK, QBLK)
-
-        def pair(p):
-            gr = pltpu.roll(gt[pl.ds(base, QBLK), :], 128 - 2 * p, 1)
-            for par, S in ((0, se), (1, so)):
-                qh = q[pl.ds(base, QBLK), pl.ds(pl.multiple_of(p * 384 + par * 128, 128), 256)]
-                ns, ds = branch(qh, S[...], sx[...], bs[...])
-                c = pl.ds(pl.multiple_of(p * 256 + par * 128, 128), DV)
-                att[:, c] = (acc[pl.ds(base, QBLK), c] + (gr[:, 8 + par : 9 + par] / ds) * ns).astype(BF)
-
-        each(lo, hi, pair)
-
-    def pr(r):
-        return remote(psend.at[r], precv.at[r], pr_s.at[r], pr_r.at[r], sib)
+        r = pl.ds(base, QBLK)
+        top = pl.ds(pl.multiple_of(core * 128, 128), 128)
+        low = pl.ds(pl.multiple_of(128 - core * 128, 128), 128)
+        for h in range(8):
+            off = (h // 2) * 384 + (h % 2) * 128
+            ns, ds = branch(q[r, off : off + 256], (so if h % 2 else se)[...], sx[...], bs[...])
+            c = slice(h * DV, (h + 1) * DV)
+            y = (acc[r, c] + (gt[r, 8 + h : 9 + h] / ds) * ns).astype(BF)
+            att[top, c] = y[:128]
+            att[low, c] = y[128:]
+
+    def pr(r, c):
+        return remote(psend.at[r, c], precv.at[r, c], pr_s.at[r, c], pr_r.at[r, c], sib)
 
     def project(r):
-        keep_rows = pl.ds(pl.multiple_of(core * 128, 128), 128)
-        give_rows = pl.ds(pl.multiple_of(128 - core * 128, 128), 128)
-        a = att[give_rows, :]
-        b = att[keep_rows, :]
-
-        def tile(i):
-            c = pl.ds(pl.multiple_of(i * 256, 256), 256)
-            psend[r, :, c] = jnp.dot(a, w[:, c], preferred_element_type=F32).astype(BF)
-            mine[r, :, c] = jnp.dot(b, w[:, c], preferred_element_type=F32)
-
-        each(0, 10, tile)
-        pr(r).start()
-
-    A = slice(0, HALF)
-    B = slice(HALF, 2 * HALF)
+        def side(i):
+            c = jnp.where(r == 1, 1 - i, i)
+            y = jnp.dot(att[...], w[:, pl.ds(pl.multiple_of(c * HALF, 128), HALF)], preferred_element_type=F32)
+            psend[r, c] = y[128:].astype(BF)
+            pr(r, c).start()
+            mine[r, c] = y[:128]
+
+        each(0, 2, side)
+
+    A, B = 0, 1
 
     def total(r, c):
-        return mine[r, :, c] + precv[r, :, c].astype(F32)
+        pr(r, c).wait_recv()
+        return mine[r, c] + precv[r, c].astype(F32)
 
     def hop_a(k):
         return remote(sa.at[k], ra.at[k], a_s.at[k], a_r.at[k], up)
@@ -325,55 +321,71 @@
     def hop_b(k):
         return remote(sb.at[k], rb.at[k], b_s.at[k], b_r.at[k], down)
 
-    order = [(x + 3) % 4, (x + 1) % 4, (x + 2) % 4, x]
-    each(0, 2, lambda r: near(jnp.where(r == 0, order[0], order[1])))
     half = me // 2
-    each(half, me, pass_on)
-    near(order[2])
-    each(0, half, pass_on)
-    loads[7].wait()
-    to_s.wait()
-    each(0, me, lambda o: fw_in(o).wait_recv())
-
-    far_setup(order[0])
-    far(order[0], 0, 4)
-    project(0)
-    far_setup(order[1])
-    far(order[1], 0, 2)
-    pr(0).wait_recv()
-    sa[0] = total(0, A).astype(BF)
-    hop_a(0).start()
-    far(order[1], 2, 4)
-    project(1)
-    far_setup(order[2])
-    far(order[2], 0, 2)
-    pr(1).wait_recv()
-    sb[0] = total(1, B).astype(BF)
-    hop_b(0).start()
-    far(order[2], 2, 4)
-    project(2)
-    near(order[3])
-    pr(2).wait_recv()
-    hop_a(0).wait_recv()
-    sa[1] = (total(2, A) + ra[0].astype(F32)).astype(BF)
-    hop_a(1).start()
-    hop_b(0).wait_recv()
-    sb[1] = (total(2, B) + rb[0].astype(F32)).astype(BF)
-    hop_b(1).start()
-    far_setup(order[3])
-    far(order[3], 0, 4)
-    hop_a(1).wait_recv()
-    sa[2] = (total(1, A) + ra[1].astype(F32)).astype(BF)
-    hop_a(2).start()
-    hop_b(1).wait_recv()
-    sb[2] = (total(0, B) + rb[1].astype(F32)).astype(BF)
-    hop_b(2).start()
-    project(3)
-    pr(3).wait_recv()
+
+    def block_of(r):
+        return (x + jnp.where(r == 0, 3, jnp.where(r == 3, 0, r))) % 4
+
+    def go(i):
+        is_near = (i < 3) | (i == 6)
+        r = jnp.where(i < 3, i, jnp.where(i < 6, i - 3, 3))
+
+        @pl.when(i == 2)
+        def _():
+            each(half, me, pass_on)
+
+        @pl.when(i == 3)
+        def _():
+            each(0, half, pass_on)
+            loads[7].wait()
+            to_s.wait()
+            each(0, me, lambda o: fw_in(o).wait_recv())
+
+        @pl.when(is_near)
+        def _():
+            near(block_of(r))
+
+        @pl.when(jnp.logical_not(is_near))
+        def _():
+            far_setup(block_of(r))
+            far(block_of(r))
+            project(r)
+
+        @pl.when(i == 3)
+        def _():
+            sa[0] = total(0, A).astype(BF)
+            hop_a(0).start()
+
+        @pl.when(i == 4)
+        def _():
+            sb[0] = total(1, B).astype(BF)
+            hop_b(0).start()
+
+        @pl.when(i == 5)
+        def _():
+            hop_a(0).wait_recv()
+            sa[1] = (total(2, A) + ra[0].astype(F32)).astype(BF)
+            hop_a(1).start()
+            hop_b(0).wait_recv()
+            sb[1] = (total(2, B) + rb[0].astype(F32)).astype(BF)
+            hop_b(1).start()
+
+        @pl.when(i == 6)
+        def _():
+            hop_a(1).wait_recv()
+            sa[2] = (total(1, A) + ra[1].astype(F32)).astype(BF)
+            hop_a(2).start()
+            hop_b(1).wait_recv()
+            sb[2] = (total(0, B) + rb[1].astype(F32)).astype(BF)
+            hop_b(2).start()
+
+    each(0, 8, go)
+    own_a = total(3, A)
     hop_a(2).wait_recv()
-    outb[:, A] = (total(3, A) + ra[2].astype(F32)).astype(BF)
+    outb[:, :HALF] = (own_a + ra[2].astype(F32)).astype(BF)
+    own_b = total(3, B)
     hop_b(2).wait_recv()
-    outb[:, B] = (total(3, B) + rb[2].astype(F32)).astype(BF)
+    outb[:, HALF:] = (own_b + rb[2].astype(F32)).astype(BF)
     done = pltpu.make_async_copy(outb, o_hbm, lsem.at[9])
     done.start()
 
@@ -387,7 +399,8 @@
         rim_c.wait_send()
 
     for r in range(4):
-        pr(r).wait_send()
+        pr(r, A).wait_send()
+        pr(r, B).wait_send()
     for k in range(3):
         hop_a(k).wait_send()
         hop_b(k).wait_send()
@@ -414,11 +427,11 @@
             V((1024, 256), BF), V((1024, 256), BF), V((1024, 256), BF),
             V((QBLK, 768), F32), V((QBLK, 512), F32), V((QBLK, 1024), F32), V((4, 8, 1024), F32),
             V((1024, 1024), F32), V((QBLK, 1024), BF),
-            V((4, 128, 2560), F32), V((4, 128, 2560), BF), V((4, 128, 2560), BF),
+            V((4, 2, 128, HALF), F32), V((4, 2, 128, HALF), BF), V((4, 2, 128, HALF), BF),
             V((3, 128, HALF), BF), V((3, 128, HALF), BF), V((3, 128, HALF), BF), V((3, 128, HALF), BF),
             V((128, 2560), BF),
             D((10,)), D((16,)), D((16,)), D((16,)), D, D, D((16,)), D((16,)), D((16,)), D((16,)), D((16,)), D((16,)),
-            D((4,)), D((4,)), D((3,)), D((3,)), D((3,)), D((3,)),
+            D((4, 2)), D((4, 2)), D((3,)), D((3,)), D((3,)), D((3,)),
         ],
         compiler_params=pltpu.CompilerParams(
             collective_id=0, has_side_effects=True, vmem_limit_bytes=60 << 20

time: 117 us -> 98.9 us (0.85)
  Pallas kernels: 114 us -> 95.4 us
    pallas_call x1, Pallas kernels: 114 us -> 95.4 us  [local(): pl.pallas_call(layer, in_specs=[hbm] * 8, out_specs=hbm, out_shape=jax.Sh...]
where the time goes in v3:
time: 98.9 us; the launch traced here: 97.3 us
  Pallas kernels  95.4 us (96%)
  local copies, waits for them, and re-layouts  1.97 us (2%)
    pallas_call x1, Pallas kernels, local(): pl.pallas_call(layer, in_specs=[hbm] * 8, out_specs=hbm, out_shape=jax.Sh...  95.4 us

profile of v3, /device:TPU:71, one launch (start us, length us, event | category | flops | bytes accessed | tf_op | source)
XLA Modules:
  0.0 97.3 jit_solution(12308763680531922469)
XLA Ops:
  0.0 95.4 %shard_map.82 = bf16[128,2560]{1,0:T(8,128)(2,1)} custom-call(bf16[1024,1536]{1,0:T(8,128)(2,1)} %q_hbm.1, bf16[1024,768]{1,0:T(8,128)(2,1)} %key_hbm.1, bf16[1024,512]{1,0:T(8,128)(2,1)} %val_hbm.1, f32[32,768]{1,0:T(8,128)} %kw_hbm.1, f32[32,512]{1,0:T(8,128)} %vw_hbm.1, s32[4,4,16]{2,1,0:T(4,128)} %picks_hbm.1, f32[24,1024]{1,0:T(8,128)} %bitcast.3, ...), custom_call_target="tpu_custom_call" | custom-call | tf_op jit(solution)/shard_map/pallas_call | solution.py:414
  95.4 2.0 %copy.10 = bf16[128,2560]{1,0:T(8,128)(2,1)} copy(bf16[128,2560]{1,0:T(8,128)(2,1)} %shard_map.82) | data formatting | bytes 1310720

commit v4 on v3

--- a/solution.py
+++ b/solution.py
@@ -145,23 +145,45 @@
     cx[:, DV:] = jnp.ones((cx.shape[0], DV), BF)
     sx[:, DV:] = jnp.ones((sx.shape[0], DV), BF)
 
-    def spread(block, rows, even_ref, odd_ref, v_ref):
-        even_ref[rows, :] = block[:, :256]
-        odd_ref[rows, :] = pltpu.roll(block[:, :256].astype(F32), 64, 1).astype(BF)
-        v_ref[rows, :DV] = block[:, 256:]
+    def spread(block, start, n, even_ref, odd_ref, v_ref):
+        r0 = pl.ds(pl.multiple_of(start, 16), n)
+        r1 = pl.ds(pl.multiple_of(start + n, 16), n)
+        wide = iota((n, 256), 1)
+        y = jnp.where(wide < QK, block[:, 0:256].astype(F32), 0.0)
+        even_ref[r0, :] = y.astype(BF)
+        odd_ref[r0, :] = pltpu.roll(y, 64, 1).astype(BF)
+        y = jnp.where(wide >= 64, block[:, 128:384].astype(F32), 0.0)
+        odd_ref[r1, :] = y.astype(BF)
+        even_ref[r1, :] = pltpu.roll(y, 192, 1).astype(BF)
+        v_ref[r0, :DV] = block[:, 384:512]
+        v_ref[r1, :DV] = block[:, 512:640]
+
+    def fold(even, odd_half, v0, v1):
+        return jnp.concatenate(
+            [even[:, :128], even[:, 128:] + odd_half[:, :128], odd_half[:, 128:], v0, v1], axis=1
+        )
 
     def pack(i):
         r = pl.ds(pl.multiple_of(i * KBLK, KBLK), KBLK)
         y = jnp.where(oddv, kbuf[r, 128:384].astype(F32), kbuf[r, 0:256].astype(F32))
         y = jnp.where(keep, y, 0.0)
-        y = jnp.where(oddv, pltpu.roll(y, 192, 1), y).astype(BF)
-        pk[i, :, :256] = y
-        pk[i, :, 256:] = vbuf[r, :]
+        turned = pltpu.roll(y, 64, 1)
+        back = pltpu.roll(y, 192, 1)
+        even = jnp.where(oddv, back, y).astype(BF)
+        odd_form = jnp.where(oddv, y, turned).astype(BF)
+        v = vbuf[r, :]
         r2 = pl.ds(pl.multiple_of(WINDOW + i * KBLK, KBLK), KBLK)
-        spread(pk[i], r2, ke, ko, vx)
-
-    each(0, 16, pack)
-    rim_c = remote(pk.at[pl.ds(8, 8)], rim, rim_s, rim_r, {"ctx": (me + 1) % n})
+        ke[r2, :] = even
+        ko[r2, :] = odd_form
+        vx[r2, :DV] = v
+        pk[i] = fold(even[:32], odd_form[32:], v[:32], v[32:])
+
+    for i in range(16):
+        pack(i)
+    rim_c = remote(
+        pk.at[pl.ds(8 + 4 * core, 4)], rim.at[pl.ds(4 * core, 4)], rim_s.at[0], rim_r.at[0], {"ctx": (me + 1) % n}
+    )
+    rim_f = remote(rim.at[pl.ds(4 * core, 4)], rim.at[pl.ds(4 * core, 4)], rim_s.at[1], rim_r.at[1], sib)
 
     @pl.when(me < n - 1)
     def _():
@@ -171,10 +193,12 @@
     wk = jnp.where(oddv[:CBLK], pltpu.roll(wk, 192, 1), wk)
     wv = vw[...]
     for b in range(32):
-        r = slice((b % 2) * 32, (b % 2) * 32 + 32)
-        crow[b : b + 1, :256] = jnp.sum(pk[b // 2, r, :256].astype(F32) * wk, axis=0, keepdims=True)
-        crow[b : b + 1, 256:] = jnp.sum(pk[b // 2, r, 256:].astype(F32) * wv, axis=0, keepdims=True)
-    cown[...] = crow[...].astype(BF)
+        r = slice(WINDOW + b * CBLK, WINDOW + (b + 1) * CBLK)
+        crow[b : b + 1, :256] = jnp.sum(ke[r, :].astype(F32) * wk, axis=0, keepdims=True)
+        crow[b : b + 1, 256:] = jnp.sum(vx[r, :DV].astype(F32) * wv, axis=0, keepdims=True)
+    c0 = crow[:16]
+    c1 = crow[16:]
+    cown[...] = fold(c0[:, :256], pltpu.roll(c1[:, :256], 64, 1), c0[:, 256:], c1[:, 256:]).astype(BF)
 
     def cp(t):
         return remote(cown, comp.at[t - me], cp_s.at[t - me], cp_r.at[t - me], {"ctx": t})
@@ -228,7 +252,7 @@
     comp[0] = cown[...]
 
     def blank(d):
-        comp[d] = jnp.zeros((CBLK, 384), BF)
+        comp[d] = jnp.zeros((16, 640), BF)
 
     each(me + 1, n, blank)
 
@@ -236,13 +260,9 @@
     def _():
         rim[...] = jnp.zeros_like(rim)
 
-    @pl.when(me > 0)
-    def _():
-        rim_c.wait_recv()
-
     each(1, me + 1, lambda d: cp_in(d).wait_recv())
-    each(0, 8, lambda i: spread(rim[i], pl.ds(pl.multiple_of(i * KBLK, KBLK), KBLK), ke, ko, vx))
-    each(0, 16, lambda i: spread(comp[i], pl.ds(pl.multiple_of(i * CBLK, CBLK), CBLK), ce, co, cx))
+    for i in range(16):
+        spread(comp[i], i * CBLK, 16, ce, co, cx)
     loads[6].wait()
     rows = iota((QBLK, QBLK), 0)
     cols = iota((QBLK, QBLK), 1)
@@ -274,11 +294,8 @@
             ) * nw
 
     def far_setup(qb):
-        def put(j):
-            r = pl.ds(pl.multiple_of(j * KBLK, KBLK), KBLK)
-            spread(blk[slots[0, qb * PICKS + j] & 63], r, se, so, sx)
-
-        each(0, PICKS, put)
+        for j in range(PICKS):
+            spread(blk[slots[0, qb * PICKS + j] & 63], j * KBLK, 32, se, so, sx)
         rs = iota((QBLK, 1024), 0)
         cs = iota((QBLK, 1024), 1)
         bs[...] = jnp.where((cs < 64) & (cs > rs), DEAD, jnp.broadcast_to(rowb[qb][0:1, :], (QBLK, 1024)))
@@ -324,11 +341,24 @@
     half = me // 2
 
     def block_of(r):
-        return (x + jnp.where(r == 0, 3, jnp.where(r == 3, 0, r))) % 4
+        return (x + jnp.where(r == 0, 2, jnp.where(r == 1, 1, jnp.where(r == 2, 3, 0)))) % 4
 
     def go(i):
         is_near = (i < 3) | (i == 6)
-        r = jnp.where(i < 3, i, jnp.where(i < 6, i - 3, 3))
+        r = jnp.where(i < 6, i - 3, 3)
+        late = jnp.where(x >= 3 - i, 2 - i, 3 - i)
+        near_block = jnp.where(i < 3, late, x)
+
+        @pl.when(i == jnp.where(x >= 2, 1, 2))
+        def _():
+            @pl.when(me > 0)
+            def _():
+                rim_c.wait_recv()
+                rim_f.start()
+                rim_f.wait_recv()
+
+            for j in range(8):
+                spread(rim[j], j * KBLK, 32, ke, ko, vx)
 
         @pl.when(i == 2)
         def _():
@@ -343,7 +373,7 @@
 
         @pl.when(is_near)
         def _():
-            near(block_of(r))
+            near(near_block)
 
         @pl.when(jnp.logical_not(is_near))
         def _():
@@ -355,37 +385,36 @@
         def _():
             sa[0] = total(0, A).astype(BF)
             hop_a(0).start()
+            sb[0] = total(0, B).astype(BF)
+            hop_b(0).start()
 
         @pl.when(i == 4)
         def _():
-            sb[0] = total(1, B).astype(BF)
-            hop_b(0).start()
+            sa[1] = total(1, B).astype(BF)
+            hop_a(1).start()
+            own = total(1, A)
+            hop_a(0).wait_recv()
+            sa[2] = (own + ra[0].astype(F32)).astype(BF)
+            hop_a(2).start()
 
         @pl.when(i == 5)
         def _():
-            hop_a(0).wait_recv()
-            sa[1] = (total(2, A) + ra[0].astype(F32)).astype(BF)
-            hop_a(1).start()
+            sb[1] = total(2, A).astype(BF)
+            hop_b(1).start()
+            own = total(2, B)
             hop_b(0).wait_recv()
-            sb[1] = (total(2, B) + rb[0].astype(F32)).astype(BF)
-            hop_b(1).start()
-
-        @pl.when(i == 6)
-        def _():
-            hop_a(1).wait_recv()
-            sa[2] = (total(1, A) + ra[1].astype(F32)).astype(BF)
-            hop_a(2).start()
-            hop_b(1).wait_recv()
-            sb[2] = (total(0, B) + rb[1].astype(F32)).astype(BF)
+            sb[2] = (own + rb[0].astype(F32)).astype(BF)
             hop_b(2).start()
 
     each(0, 8, go)
     own_a = total(3, A)
     hop_a(2).wait_recv()
-    outb[:, :HALF] = (own_a + ra[2].astype(F32)).astype(BF)
+    hop_b(1).wait_recv()
+    outb[:, :HALF] = (own_a + ra[2].astype(F32) + rb[1].astype(F32)).astype(BF)
     own_b = total(3, B)
+    hop_a(1).wait_recv()
     hop_b(2).wait_recv()
-    outb[:, HALF:] = (own_b + rb[2].astype(F32)).astype(BF)
+    outb[:, HALF:] = (own_b + ra[1].astype(F32) + rb[2].astype(F32)).astype(BF)
     done = pltpu.make_async_copy(outb, o_hbm, lsem.at[9])
     done.start()
 
@@ -397,6 +426,10 @@
     @pl.when(me < n - 1)
     def _():
         rim_c.wait_send()
+
+    @pl.when(me > 0)
+    def _():
+        rim_f.wait_send()
 
     for r in range(4):
         pr(r, A).wait_send()
@@ -419,9 +452,9 @@
         scratch_shapes=[
             V((1024, 1536), BF), V((1024, 384), BF), V((1024, DV), BF), V((CBLK, 384), F32), V((CBLK, DV), F32),
             V((4, 4, PICKS), I32), V((24, 1024), F32), V((1024, 2560), BF), V((1024, 128), F32),
-            V((16, 64, 384), BF), V((32, 384), F32), V((32, 384), BF), V((8, 128), I32), V((16, 8, 128), I32),
+            V((16, 32, 640), BF), V((32, 384), F32), V((16, 640), BF), V((8, 128), I32), V((16, 8, 128), I32),
             pltpu.SMEM((16, 8, 128), I32), V((8, 128), I32), pltpu.SMEM((8, 128), I32),
-            V((16, 2, 64, 384), BF), V((64, 64, 384), BF), V((16, 32, 384), BF), V((8, 64, 384), BF),
+            V((16, 2, 32, 640), BF), V((64, 32, 640), BF), V((16, 16, 640), BF), V((8, 32, 640), BF),
             V((1536, 256), BF), V((1536, 256), BF), V((1536, 256), BF),
             V((512, 256), BF), V((512, 256), BF), V((512, 256), BF),
             V((1024, 256), BF), V((1024, 256), BF), V((1024, 256), BF),
@@ -430,7 +463,7 @@
             V((4, 2, 128, HALF), F32), V((4, 2, 128, HALF), BF), V((4, 2, 128, HALF), BF),
             V((3, 128, HALF), BF), V((3, 128, HALF), BF), V((3, 128, HALF), BF), V((3, 128, HALF), BF),
             V((128, 2560), BF),
-            D((10,)), D((16,)), D((16,)), D((16,)), D, D, D((16,)), D((16,)), D((16,)), D((16,)), D((16,)), D((16,)),
+            D((10,)), D((16,)), D((16,)), D((16,)), D((2,)), D((2,)), D((16,)), D((16,)), D((16,)), D((16,)), D((16,)), D((16,)),
             D((4, 2)), D((4, 2)), D((3,)), D((3,)), D((3,)), D((3,)),
         ],
         compiler_params=pltpu.CompilerParams(

time: 98.9 us -> 85.8 us (0.87); the launches traced: 97.3 us -> 85.6 us
  Pallas kernels: 95.4 us -> 83.7 us
    pallas_call x1, Pallas kernels: 95.4 us -> 83.7 us  [local(): pl.pallas_call(layer, in_specs=[hbm] * 8, out_specs=hbm, out_shape=jax.Sh...]
where the time goes in v4:
time: 85.8 us; the launch traced here: 85.6 us
  Pallas kernels  83.7 us (98%)
  local copies, waits for them, and re-layouts  1.97 us (2%)
    pallas_call x1, Pallas kernels, local(): pl.pallas_call(layer, in_specs=[hbm] * 8, out_specs=hbm, out_shape=jax.Sh...  83.7 us
    unnamed x1, local copies, waits for them, and re-layouts  1.97 us

profile of v4, /device:TPU:71, one launch (start us, length us, event | category | flops | bytes accessed | tf_op | source)
XLA Modules:
  0.0 85.6 jit_solution(17015006166854982829)
XLA Ops:
  0.0 83.7 %shard_map.82 = bf16[128,2560]{1,0:T(8,128)(2,1)} custom-call(bf16[1024,1536]{1,0:T(8,128)(2,1)} %q_hbm.1, bf16[1024,768]{1,0:T(8,128)(2,1)} %key_hbm.1, bf16[1024,512]{1,0:T(8,128)(2,1)} %val_hbm.1, f32[32,768]{1,0:T(8,128)} %kw_hbm.1, f32[32,512]{1,0:T(8,128)} %vw_hbm.1, s32[4,4,16]{2,1,0:T(4,128)} %picks_hbm.1, f32[24,1024]{1,0:T(8,128)} %bitcast.3, ...), custom_call_target="tpu_custom_call" | custom-call | tf_op jit(solution)/shard_map/pallas_call | solution.py:447
  83.7 2.0 %copy.10 = bf16[128,2560]{1,0:T(8,128)(2,1)} copy(bf16[128,2560]{1,0:T(8,128)(2,1)} %shard_map.82) | data formatting | bytes 1310720

commit v5 on v4

--- a/solution.py
+++ b/solution.py
@@ -77,7 +77,7 @@
     q_hbm, key_hbm, val_hbm, kw_hbm, vw_hbm, picks_hbm, gate_hbm, w_hbm, o_hbm,
     q, kbuf, vbuf, kw, vw, picks, gate, w, gt,
     pk, crow, cown, reqb, reqin, reqs, slotb, slots, send, blk, comp, rim,
-    ke, ko, vx, ce, co, cx, se, so, sx, bw, bc, bs, rowb, acc, att,
+    ke, ko, vx, ce, co, cx, se, so, sx, bw, bc, bs, rowb, acc, accc, att,
     mine, psend, precv, sa, ra, sb, rb, outb,
     lsem, sm_s, rq_s, rq_r, rim_s, rim_r, cp_s, cp_r, bk_s, bk_r, fw_s, fw_r, pr_s, pr_r, a_s, a_r, b_s, b_r,
 ):
@@ -185,10 +185,6 @@
     )
     rim_f = remote(rim.at[pl.ds(4 * core, 4)], rim.at[pl.ds(4 * core, 4)], rim_s.at[1], rim_r.at[1], sib)
 
-    @pl.when(me < n - 1)
-    def _():
-        rim_c.start()
-
     wk = jnp.where(oddv[:CBLK], kw[:, 128:384], kw[:, 0:256])
     wk = jnp.where(oddv[:CBLK], pltpu.roll(wk, 192, 1), wk)
     wv = vw[...]
@@ -208,6 +204,10 @@
 
     each(me + 1, n, lambda t: cp(t).start())
 
+    @pl.when(me < n - 1)
+    def _():
+        rim_c.start()
+
     def sm(t):
         return pltpu.make_async_copy(reqin.at[t], reqs.at[t], sm_s.at[t])
 
@@ -260,19 +260,25 @@
     def _():
         rim[...] = jnp.zeros_like(rim)
 
-    each(1, me + 1, lambda d: cp_in(d).wait_recv())
-    for i in range(16):
-        spread(comp[i], i * CBLK, 16, ce, co, cx)
     loads[6].wait()
     rows = iota((QBLK, QBLK), 0)
     cols = iota((QBLK, QBLK), 1)
 
-    def near(qb):
+    def window(qb):
         base = pl.multiple_of(qb * QBLK, QBLK)
         first = me * 1024 + base
         bw[:, :256] = jnp.where(cols >= rows, jnp.where(first < 512, DEAD, 0.0), DEAD)
         bw[:, 256:512] = jnp.full((QBLK, QBLK), jnp.where(first < 256, DEAD, 0.0))
         bw[:, 512:] = jnp.where(cols <= rows, 0.0, DEAD)
+        r = pl.ds(base, QBLK)
+        span = pl.ds(base, 768)
+        for h in range(8):
+            off = (h // 2) * 384 + (h % 2) * 128
+            nw, dw = branch(q[r, off : off + 256], (ko if h % 2 else ke)[span, :], vx[span, :], bw[...])
+            acc[r, h * DV : (h + 1) * DV] = (gt[r, 16 + h : 17 + h] / dw) * nw
+
+    def compressed(qb):
+        base = pl.multiple_of(qb * QBLK, QBLK)
         rowc = iota((QBLK, 512), 0)
         colc = iota((QBLK, 512), 1)
         bc[...] = jnp.where(
@@ -280,18 +286,11 @@
             jnp.where(colc * 32 + 31 <= base + rowc, 0.0, DEAD),
             jnp.where(colc < (me + 1) * 32, 0.0, DEAD),
         )
-
         r = pl.ds(base, QBLK)
-        span = pl.ds(base, 768)
         for h in range(8):
             off = (h // 2) * 384 + (h % 2) * 128
-            qh = q[r, off : off + 256]
-            K, C = (ko, co) if h % 2 else (ke, ce)
-            nc, dc = branch(qh, C[...], cx[...], bc[...])
-            nw, dw = branch(qh, K[span, :], vx[span, :], bw[...])
-            acc[r, h * DV : (h + 1) * DV] = (gt[r, h : h + 1] / jnp.maximum(dc, 1.0)) * nc + (
-                gt[r, 16 + h : 17 + h] / dw
-            ) * nw
+            nc, dc = branch(q[r, off : off + 256], (co if h % 2 else ce)[...], cx[...], bc[...])
+            accc[r, h * DV : (h + 1) * DV] = (gt[r, h : h + 1] / jnp.maximum(dc, 1.0)) * nc
 
     def far_setup(qb):
         for j in range(PICKS):
@@ -309,7 +308,7 @@
             off = (h // 2) * 384 + (h % 2) * 128
             ns, ds = branch(q[r, off : off + 256], (so if h % 2 else se)[...], sx[...], bs[...])
             c = slice(h * DV, (h + 1) * DV)
-            y = (acc[r, c] + (gt[r, 8 + h : 9 + h] / ds) * ns).astype(BF)
+            y = (acc[r, c] + accc[r, c] + (gt[r, 8 + h : 9 + h] / ds) * ns).astype(BF)
             att[top, c] = y[:128]
             att[low, c] = y[128:]
 
@@ -338,75 +337,105 @@
     def hop_b(k):
         return remote(sb.at[k], rb.at[k], b_s.at[k], b_r.at[k], down)
 
-    half = me // 2
-
     def block_of(r):
         return (x + jnp.where(r == 0, 2, jnp.where(r == 1, 1, jnp.where(r == 2, 3, 0)))) % 4
 
+    def late(k):
+        return jnp.where(x >= 3 - k, 2 - k, 3 - k)
+
+    def ship0():
+        sa[0] = total(0, A).astype(BF)
+        hop_a(0).start()
+        sb[0] = total(0, B).astype(BF)
+        hop_b(0).start()
+
+    def ship1():
+        sa[1] = total(1, B).astype(BF)
+        hop_a(1).start()
+        own = total(1, A)
+        hop_a(0).wait_recv()
+        sa[2] = (own + ra[0].astype(F32)).astype(BF)
+        hop_a(2).start()
+
+    def ship2():
+        sb[1] = total(2, A).astype(BF)
+        hop_b(1).start()
+        own = total(2, B)
+        hop_b(0).wait_recv()
+        sb[2] = (own + rb[0].astype(F32)).astype(BF)
+        hop_b(2).start()
+
+    third = me // 3
+
     def go(i):
-        is_near = (i < 3) | (i == 6)
-        r = jnp.where(i < 6, i - 3, 3)
-        late = jnp.where(x >= 3 - i, 2 - i, 3 - i)
-        near_block = jnp.where(i < 3, late, x)
-
-        @pl.when(i == jnp.where(x >= 2, 1, 2))
+        is_w = (i == 0) | (i == 4) | (i == 5) | (i == 9)
+        is_c = ((i >= 1) & (i <= 3)) | (i == 10)
+        is_f = ((i >= 6) & (i <= 8)) | (i == 11)
+        w_block = jnp.where(i == 9, x, late(jnp.where(i == 0, 0, i - 3)))
+        c_block = jnp.where(i == 10, x, late(i - 1))
+        r = jnp.where(i == 11, 3, i - 6)
+
+        @pl.when(i == 1)
+        def _():
+            each(1, me + 1, lambda d: cp_in(d).wait_recv())
+            for k in range(16):
+                spread(comp[k], k * CBLK, 16, ce, co, cx)
+
+        @pl.when(i == 4)
         def _():
             @pl.when(me > 0)
             def _():
                 rim_c.wait_recv()
                 rim_f.start()
+
+            each(2 * third, me, pass_on)
+
+            @pl.when(me > 0)
+            def _():
                 rim_f.wait_recv()
 
             for j in range(8):
                 spread(rim[j], j * KBLK, 32, ke, ko, vx)
 
-        @pl.when(i == 2)
-        def _():
-            each(half, me, pass_on)
-
-        @pl.when(i == 3)
-        def _():
-            each(0, half, pass_on)
+        @pl.when(i == 5)
+        def _():
+            each(third, 2 * third, pass_on)
+
+        @pl.when(i == 6)
+        def _():
+            each(0, third, pass_on)
             loads[7].wait()
             to_s.wait()
             each(0, me, lambda o: fw_in(o).wait_recv())
 
-        @pl.when(is_near)
-        def _():
-            near(near_block)
-
-        @pl.when(jnp.logical_not(is_near))
+        @pl.when(is_w)
+        def _():
+            window(w_block)
+
+        @pl.when(is_c)
+        def _():
+            compressed(c_block)
+
+        @pl.when(is_f)
         def _():
             far_setup(block_of(r))
+
+            @pl.when(i == 7)
+            def _():
+                ship0()
+
+            @pl.when(i == 8)
+            def _():
+                ship1()
+
             far(block_of(r))
             project(r)
 
-        @pl.when(i == 3)
-        def _():
-            sa[0] = total(0, A).astype(BF)
-            hop_a(0).start()
-            sb[0] = total(0, B).astype(BF)
-            hop_b(0).start()
-
-        @pl.when(i == 4)
-        def _():
-            sa[1] = total(1, B).astype(BF)
-            hop_a(1).start()
-            own = total(1, A)
-            hop_a(0).wait_recv()
-            sa[2] = (own + ra[0].astype(F32)).astype(BF)
-            hop_a(2).start()
-
-        @pl.when(i == 5)
-        def _():
-            sb[1] = total(2, A).astype(BF)
-            hop_b(1).start()
-            own = total(2, B)
-            hop_b(0).wait_recv()
-            sb[2] = (own + rb[0].astype(F32)).astype(BF)
-            hop_b(2).start()
-
-    each(0, 8, go)
+        @pl.when(i == 8)
+        def _():
+            ship2()
+
+    each(0, 12, go)
     own_a = total(3, A)
     hop_a(2).wait_recv()
     hop_b(1).wait_recv()
@@ -459,7 +488,7 @@
             V((512, 256), BF), V((512, 256), BF), V((512, 256), BF),
             V((1024, 256), BF), V((1024, 256), BF), V((1024, 256), BF),
             V((QBLK, 768), F32), V((QBLK, 512), F32), V((QBLK, 1024), F32), V((4, 8, 1024), F32),
-            V((1024, 1024), F32), V((QBLK, 1024), BF),
+            V((1024, 1024), F32), V((1024, 1024), F32), V((QBLK, 1024), BF),
             V((4, 2, 128, HALF), F32), V((4, 2, 128, HALF), BF), V((4, 2, 128, HALF), BF),
             V((3, 128, HALF), BF), V((3, 128, HALF), BF), V((3, 128, HALF), BF), V((3, 128, HALF), BF),
             V((128, 2560), BF),

time: 85.8 us -> 82.8 us (0.965)
  Pallas kernels: 83.7 us -> 80.7 us
    pallas_call x1, Pallas kernels: 83.7 us -> 80.7 us  [local(): pl.pallas_call(layer, in_specs=[hbm] * 8, out_specs=hbm, out_shape=jax.Sh...]
where the time goes in v5:
time: 82.8 us; the launch traced here: 82.7 us
  Pallas kernels  80.7 us (97%)
  local copies, waits for them, and re-layouts  1.97 us (2%)
    pallas_call x1, Pallas kernels, local(): pl.pallas_call(layer, in_specs=[hbm] * 8, out_specs=hbm, out_shape=jax.Sh...  80.7 us
    unnamed x1, local copies, waits for them, and re-layouts  1.97 us

profile of v5, /device:TPU:71, one launch (start us, length us, event | category | flops | bytes accessed | tf_op | source)
XLA Modules:
  0.0 82.7 jit_solution(16309529692786761256)
XLA Ops:
  0.0 80.7 %shard_map.82 = bf16[128,2560]{1,0:T(8,128)(2,1)} custom-call(bf16[1024,1536]{1,0:T(8,128)(2,1)} %q_hbm.1, bf16[1024,768]{1,0:T(8,128)(2,1)} %key_hbm.1, bf16[1024,512]{1,0:T(8,128)(2,1)} %val_hbm.1, f32[32,768]{1,0:T(8,128)} %kw_hbm.1, f32[32,512]{1,0:T(8,128)} %vw_hbm.1, s32[4,4,16]{2,1,0:T(4,128)} %picks_hbm.1, f32[24,1024]{1,0:T(8,128)} %bitcast.3, ...), custom_call_target="tpu_custom_call" | custom-call | tf_op jit(solution)/shard_map/pallas_call | solution.py:476
  80.7 2.0 %copy.10 = bf16[128,2560]{1,0:T(8,128)(2,1)} copy(bf16[128,2560]{1,0:T(8,128)(2,1)} %shard_map.82) | data formatting | bytes 1310720

commit v6 on v5

--- a/solution.py
+++ b/solution.py
@@ -368,34 +368,36 @@
     third = me // 3
 
     def go(i):
-        is_w = (i == 0) | (i == 4) | (i == 5) | (i == 9)
-        is_c = ((i >= 1) & (i <= 3)) | (i == 10)
+        is_w = (i <= 2) | (i == 9)
+        is_c = ((i >= 3) & (i <= 5)) | (i == 10)
         is_f = ((i >= 6) & (i <= 8)) | (i == 11)
-        w_block = jnp.where(i == 9, x, late(jnp.where(i == 0, 0, i - 3)))
-        c_block = jnp.where(i == 10, x, late(i - 1))
+        w_block = jnp.where(i == 9, x, late(i))
+        c_block = jnp.where(i == 10, x, late(i - 3))
         r = jnp.where(i == 11, 3, i - 6)
 
-        @pl.when(i == 1)
+        @pl.when(i == 3)
         def _():
             each(1, me + 1, lambda d: cp_in(d).wait_recv())
             for k in range(16):
                 spread(comp[k], k * CBLK, 16, ce, co, cx)
 
-        @pl.when(i == 4)
+        @pl.when(i == jnp.where(x >= 2, 1, 2))
         def _():
             @pl.when(me > 0)
             def _():
                 rim_c.wait_recv()
                 rim_f.start()
 
-            each(2 * third, me, pass_on)
-
             @pl.when(me > 0)
             def _():
                 rim_f.wait_recv()
 
             for j in range(8):
                 spread(rim[j], j * KBLK, 32, ke, ko, vx)
+
+        @pl.when(i == 4)
+        def _():
+            each(2 * third, me, pass_on)
 
         @pl.when(i == 5)
         def _():

time: 82.8 us -> 76 us (0.918)
  Pallas kernels: 80.7 us -> 73.9 us
    pallas_call x1, Pallas kernels: 80.7 us -> 73.9 us  [local(): pl.pallas_call(layer, in_specs=[hbm] * 8, out_specs=hbm, out_shape=jax.Sh...]
where the time goes in v6:
time: 76 us; the launch traced here: 75.9 us
  Pallas kernels  73.9 us (97%)
  local copies, waits for them, and re-layouts  1.97 us (3%)
    pallas_call x1, Pallas kernels, local(): pl.pallas_call(layer, in_specs=[hbm] * 8, out_specs=hbm, out_shape=jax.Sh...  73.9 us
    unnamed x1, local copies, waits for them, and re-layouts  1.97 us

profile of v6, /device:TPU:71, one launch (start us, length us, event | category | flops | bytes accessed | tf_op | source)
XLA Modules:
  0.0 75.9 jit_solution(10543431747591751136)
XLA Ops:
  0.0 73.9 %shard_map.82 = bf16[128,2560]{1,0:T(8,128)(2,1)} custom-call(bf16[1024,1536]{1,0:T(8,128)(2,1)} %q_hbm.1, bf16[1024,768]{1,0:T(8,128)(2,1)} %key_hbm.1, bf16[1024,512]{1,0:T(8,128)(2,1)} %val_hbm.1, f32[32,768]{1,0:T(8,128)} %kw_hbm.1, f32[32,512]{1,0:T(8,128)} %vw_hbm.1, s32[4,4,16]{2,1,0:T(4,128)} %picks_hbm.1, f32[24,1024]{1,0:T(8,128)} %bitcast.3, ...), custom_call_target="tpu_custom_call" | custom-call | tf_op jit(solution)/shard_map/pallas_call | solution.py:478
  73.9 2.0 %copy.10 = bf16[128,2560]{1,0:T(8,128)(2,1)} copy(bf16[128,2560]{1,0:T(8,128)(2,1)} %shard_map.82) | data formatting | bytes 1310720

commit v7 on v6

--- a/solution.py
+++ b/solution.py
@@ -65,6 +65,15 @@
     return acc[:, :DV], acc[:, DV:]
 
 
+def named_branch(q, k, v, tri, row):
+    s = lax.dot_general(q, k, (((1,), (1,)), ((), ())), preferred_element_type=F32)
+    s = jnp.concatenate([s[:, :128] + tri, s[:, 128:] + row], axis=1)
+    top = jnp.maximum(jnp.max(s, axis=1, keepdims=True), FLOOR)
+    w = jnp.exp2((s - top) * SCALE2).astype(BF)
+    acc = jnp.dot(w, v, preferred_element_type=F32)
+    return acc[:, :DV], acc[:, DV:]
+
+
 def each(lo, hi, act):
     def step(i, carry):
         act(i)
@@ -185,6 +194,10 @@
     )
     rim_f = remote(rim.at[pl.ds(4 * core, 4)], rim.at[pl.ds(4 * core, 4)], rim_s.at[1], rim_r.at[1], sib)
 
+    @pl.when(me < n - 1)
+    def _():
+        rim_c.start()
+
     wk = jnp.where(oddv[:CBLK], kw[:, 128:384], kw[:, 0:256])
     wk = jnp.where(oddv[:CBLK], pltpu.roll(wk, 192, 1), wk)
     wv = vw[...]
@@ -204,10 +217,6 @@
 
     each(me + 1, n, lambda t: cp(t).start())
 
-    @pl.when(me < n - 1)
-    def _():
-        rim_c.start()
-
     def sm(t):
         return pltpu.make_async_copy(reqin.at[t], reqs.at[t], sm_s.at[t])
 
@@ -215,7 +224,6 @@
         rq_in(t).wait_recv()
         sm(t).start()
 
-    each(me + 1, n, take)
 
     def bk(t):
         return remote(send.at[t], blk.at[pl.ds(me * 4 + 2 * core, 2)], bk_s.at[t], bk_r.at[me], {"ctx": t})
@@ -237,7 +245,6 @@
             send[t, j] = pk[reqs[t, 0, me * 4 + 2 * core + j] & 15]
         bk(t).start()
 
-    each(me + 1, n, give)
 
     def pass_on(o):
         bk_in(o).wait_recv()
@@ -295,9 +302,9 @@
     def far_setup(qb):
         for j in range(PICKS):
             spread(blk[slots[0, qb * PICKS + j] & 63], j * KBLK, 32, se, so, sx)
-        rs = iota((QBLK, 1024), 0)
-        cs = iota((QBLK, 1024), 1)
-        bs[...] = jnp.where((cs < 64) & (cs > rs), DEAD, jnp.broadcast_to(rowb[qb][0:1, :], (QBLK, 1024)))
+        rs = iota((QBLK, 128), 0)
+        cs = iota((QBLK, 128), 1)
+        bs[...] = jnp.where((cs < 64) & (cs > rs), DEAD, jnp.broadcast_to(rowb[qb][0:1, :128], (QBLK, 128)))
 
     def far(qb):
         base = pl.multiple_of(qb * QBLK, QBLK)
@@ -306,7 +313,9 @@
         low = pl.ds(pl.multiple_of(128 - core * 128, 128), 128)
         for h in range(8):
             off = (h // 2) * 384 + (h % 2) * 128
-            ns, ds = branch(q[r, off : off + 256], (so if h % 2 else se)[...], sx[...], bs[...])
+            ns, ds = named_branch(
+                q[r, off : off + 256], (so if h % 2 else se)[...], sx[...], bs[...], rowb[qb][0:1, 128:]
+            )
             c = slice(h * DV, (h + 1) * DV)
             y = (acc[r, c] + accc[r, c] + (gt[r, 8 + h : 9 + h] / ds) * ns).astype(BF)
             att[top, c] = y[:128]
@@ -360,28 +369,33 @@
     def ship2():
         sb[1] = total(2, A).astype(BF)
         hop_b(1).start()
+
+    def ship3():
         own = total(2, B)
         hop_b(0).wait_recv()
         sb[2] = (own + rb[0].astype(F32)).astype(BF)
         hop_b(2).start()
 
     third = me // 3
+    early = (me % 4 == 0) & (me > 0) & (x >= 2)
 
     def go(i):
-        is_w = (i <= 2) | (i == 9)
-        is_c = ((i >= 3) & (i <= 5)) | (i == 10)
-        is_f = ((i >= 6) & (i <= 8)) | (i == 11)
-        w_block = jnp.where(i == 9, x, late(i))
-        c_block = jnp.where(i == 10, x, late(i - 3))
-        r = jnp.where(i == 11, 3, i - 6)
-
-        @pl.when(i == 3)
+        is_w = (i <= 2) | ((i == 3) & early) | ((i == 10) & jnp.logical_not(early))
+        is_c = ((i >= 4) & (i <= 6)) | (i == 11)
+        is_f = ((i >= 7) & (i <= 9)) | (i == 12)
+        w_block = jnp.where(
+            (i == 10) | ((i == 1) & early), x, late(jnp.where(early & (i >= 2), i - 1, i))
+        )
+        c_block = jnp.where(i == 11, x, late(i - 4))
+        r = jnp.where(i == 12, 3, i - 7)
+
+        @pl.when(i == 4)
         def _():
             each(1, me + 1, lambda d: cp_in(d).wait_recv())
             for k in range(16):
                 spread(comp[k], k * CBLK, 16, ce, co, cx)
 
-        @pl.when(i == jnp.where(x >= 2, 1, 2))
+        @pl.when(i == jnp.where((x >= 2) & jnp.logical_not(early), 1, 2))
         def _():
             @pl.when(me > 0)
             def _():
@@ -395,15 +409,15 @@
             for j in range(8):
                 spread(rim[j], j * KBLK, 32, ke, ko, vx)
 
-        @pl.when(i == 4)
+        @pl.when(i == 5)
         def _():
             each(2 * third, me, pass_on)
 
-        @pl.when(i == 5)
+        @pl.when(i == 6)
         def _():
             each(third, 2 * third, pass_on)
 
-        @pl.when(i == 6)
+        @pl.when(i == 7)
         def _():
             each(0, third, pass_on)
             loads[7].wait()
@@ -414,6 +428,11 @@
         def _():
             window(w_block)
 
+        @pl.when(i == 0)
+        def _():
+            each(me + 1, n, take)
+            each(me + 1, n, give)
+
         @pl.when(is_c)
         def _():
             compressed(c_block)
@@ -422,22 +441,26 @@
         def _():
             far_setup(block_of(r))
 
-            @pl.when(i == 7)
+            @pl.when(i == 8)
             def _():
                 ship0()
 
-            @pl.when(i == 8)
+            @pl.when(i == 9)
             def _():
                 ship1()
 
             far(block_of(r))
             project(r)
 
-        @pl.when(i == 8)
+        @pl.when(i == 9)
         def _():
             ship2()
 
-    each(0, 12, go)
+        @pl.when(i == 10)
+        def _():
+            ship3()
+
+    each(0, 13, go)
     own_a = total(3, A)
     hop_a(2).wait_recv()
     hop_b(1).wait_recv()
@@ -489,7 +512,7 @@
             V((1536, 256), BF), V((1536, 256), BF), V((1536, 256), BF),
             V((512, 256), BF), V((512, 256), BF), V((512, 256), BF),
             V((1024, 256), BF), V((1024, 256), BF), V((1024, 256), BF),
-            V((QBLK, 768), F32), V((QBLK, 512), F32), V((QBLK, 1024), F32), V((4, 8, 1024), F32),
+            V((QBLK, 768), F32), V((QBLK, 512), F32), V((QBLK, 128), F32), V((4, 8, 1024), F32),
             V((1024, 1024), F32), V((1024, 1024), F32), V((QBLK, 1024), BF),
             V((4, 2, 128, HALF), F32), V((4, 2, 128, HALF), BF), V((4, 2, 128, HALF), BF),
             V((3, 128, HALF), BF), V((3, 128, HALF), BF), V((3, 128, HALF), BF), V((3, 128, HALF), BF),

time: 76 us -> 75.9 us (level)
  no operation moved by 1% of the time
where the time goes in v7:
time: 75.9 us; the launch traced here: 75.8 us
  Pallas kernels  73.8 us (97%)
  local copies, waits for them, and re-layouts  1.97 us (3%)
    pallas_call x1, Pallas kernels, local(): pl.pallas_call(layer, in_specs=[hbm] * 8, out_specs=hbm, out_shape=jax.Sh...  73.8 us
    unnamed x1, local copies, waits for them, and re-layouts  1.97 us

profile of v7, /device:TPU:71, one launch (start us, length us, event | category | flops | bytes accessed | tf_op | source)
XLA Modules:
  0.0 75.8 jit_solution(9476972378211780904)
XLA Ops:
  0.0 73.8 %shard_map.82 = bf16[128,2560]{1,0:T(8,128)(2,1)} custom-call(bf16[1024,1536]{1,0:T(8,128)(2,1)} %q_hbm.1, bf16[1024,768]{1,0:T(8,128)(2,1)} %key_hbm.1, bf16[1024,512]{1,0:T(8,128)(2,1)} %val_hbm.1, f32[32,768]{1,0:T(8,128)} %kw_hbm.1, f32[32,512]{1,0:T(8,128)} %vw_hbm.1, s32[4,4,16]{2,1,0:T(4,128)} %picks_hbm.1, f32[24,1024]{1,0:T(8,128)} %bitcast.3, ...), custom_call_target="tpu_custom_call" | custom-call | tf_op jit(solution)/shard_map/pallas_call | solution.py:501
  73.8 2.0 %copy.10 = bf16[128,2560]{1,0:T(8,128)(2,1)} copy(bf16[128,2560]{1,0:T(8,128)(2,1)} %shard_map.82) | data formatting | bytes 1310720

commit v8 on v7

--- a/solution.py
+++ b/solution.py
@@ -376,7 +376,8 @@
         sb[2] = (own + rb[0].astype(F32)).astype(BF)
         hop_b(2).start()
 
-    third = me // 3
+    cut1 = jnp.where(me % 4 == 0, me, 2 * (me // 3))
+    cut2 = jnp.where(me % 4 == 0, me, me // 3)
     early = (me % 4 == 0) & (me > 0) & (x >= 2)
 
     def go(i):
@@ -411,15 +412,15 @@
 
         @pl.when(i == 5)
         def _():
-            each(2 * third, me, pass_on)
+            each(cut1, me, pass_on)
 
         @pl.when(i == 6)
         def _():
-            each(third, 2 * third, pass_on)
+            each(cut2, cut1, pass_on)
 
         @pl.when(i == 7)
         def _():
-            each(0, third, pass_on)
+            each(0, cut2, pass_on)
             loads[7].wait()
             to_s.wait()
             each(0, me, lambda o: fw_in(o).wait_recv())

time: 75.9 us -> 76.6 us (level)
  no operation moved by 1% of the time
where the time goes in v8:
time: 76.6 us; the launch traced here: 76.4 us
  Pallas kernels  74.4 us (97%)
  local copies, waits for them, and re-layouts  1.97 us (3%)
    pallas_call x1, Pallas kernels, local(): pl.pallas_call(layer, in_specs=[hbm] * 8, out_specs=hbm, out_shape=jax.Sh...  74.4 us
    unnamed x1, local copies, waits for them, and re-layouts  1.97 us

profile of v8, /device:TPU:71, one launch (start us, length us, event | category | flops | bytes accessed | tf_op | source)
XLA Modules:
  0.0 76.4 jit_solution(15681392059622809082)
XLA Ops:
  0.0 74.4 %shard_map.82 = bf16[128,2560]{1,0:T(8,128)(2,1)} custom-call(bf16[1024,1536]{1,0:T(8,128)(2,1)} %q_hbm.1, bf16[1024,768]{1,0:T(8,128)(2,1)} %key_hbm.1, bf16[1024,512]{1,0:T(8,128)(2,1)} %val_hbm.1, f32[32,768]{1,0:T(8,128)} %kw_hbm.1, f32[32,512]{1,0:T(8,128)} %vw_hbm.1, s32[4,4,16]{2,1,0:T(4,128)} %picks_hbm.1, f32[24,1024]{1,0:T(8,128)} %bitcast.3, ...), custom_call_target="tpu_custom_call" | custom-call | tf_op jit(solution)/shard_map/pallas_call | solution.py:502
  74.5 2.0 %copy.10 = bf16[128,2560]{1,0:T(8,128)(2,1)} copy(bf16[128,2560]{1,0:T(8,128)(2,1)} %shard_map.82) | data formatting | bytes 1310720
